TPU v7x, 32 devices: a whole 2x2x4 slice. The times are simulated.
32 devices in a mesh: groups: 2 (over y), lon: 4 (over z), lat: 2 (over x), dp: 2 (over core).
Axes of the slice: x: 2, y: 2, z: 4, core: 2. Of those that a mesh axis runs over, the one named last changes fastest.
Arguments:
- fields: bfloat16 [4, 32, 64, 192], P(('groups', 'dp'), 'lat', 'lon'), parts along dimension 0, may hold values from -6 to 6
- cotangent: bfloat16 [4, 32, 64, 192], P(('groups', 'dp'), 'lat', 'lon'), parts along dimension 0, may hold values from -6 to 6
- ocean_mask: int32 [32, 64], P('lat', 'lon'), may hold values from 0 to 1, as said below
- dw_kernel: float32 [7, 7, 192], replicated, may hold values from -0.875 to 0.875
- dw_bias: float32 [192], replicated, may hold values from -4 to 4
- ln_gain: float32 [192], replicated, may hold values from 0.1 to 1.9
- ln_bias: float32 [192], replicated, may hold values from -3 to 3
- w_in: bfloat16 [192, 768], replicated, may hold values from -0.4375 to 0.4375
- b_in: float32 [768], replicated, may hold values from -3 to 3
- w_out: bfloat16 [768, 192], replicated, may hold values from -0.21875 to 0.21875
- b_out: float32 [192], replicated, may hold values from -3 to 3
- layer_scale: float32 [192], replicated, may hold values from 0.3 to 1.5
Outputs:
- block_out: bfloat16 [4, 32, 64, 192], P(('groups', 'dp'), 'lat', 'lon'), parts along dimension 0
- field_grad: bfloat16 [4, 32, 64, 192], P(('groups', 'dp'), 'lat', 'lon'), parts along dimension 0
- grad_kernel: float32 [14, 7, 192], P('groups'), parts along dimension 0
- grad_dw_bias: float32 [384], P('groups'), parts along dimension 0
- grad_ln_gain: float32 [384], P('groups'), parts along dimension 0
- grad_ln_bias: float32 [384], P('groups'), parts along dimension 0
- grad_w_in: float32 [384, 768], P('groups'), parts along dimension 0
- grad_b_in: float32 [1536], P('groups'), parts along dimension 0
- grad_w_out: float32 [1536, 192], P('groups'), parts along dimension 0
- grad_b_out: float32 [384], P('groups'), parts along dimension 0
- grad_scale: float32 [384], P('groups'), parts along dimension 0
There are 2 independent parts, one for each index of `groups`. A program takes and returns all parts, laid end to end along the dimension named above; an argument that names none is the same for every part. Nothing has to cross between parts.
Inputs may be any that keep to these rules, and one draw needn't show every extreme that they name: `ocean_mask`: each device's tile of 16 x 16 cells holds at most 192 ocean cells, and some tile holds exactly 192.
All inputs are finite; a program needn't handle non-finite values.
Results may differ from a plain program's by a relative error of at most 0.0065.
Values may be sent and summed in bfloat16 or wider, within the bound.
No kernel may reach another device: no remote copies, remote signals or barrier semaphores. Data moves between devices by JAX's collectives and lax.ppermute only.
A program may use at most 64 MiB of HBM per device.

v0:
```python
import math

import jax
import jax.numpy as jnp
from jax import lax
from jax.sharding import PartitionSpec as P

EPS = 1e-06


def padded_2(block, sides, width, periodic):
    for axis, dim in sides:
        count = lax.axis_size(axis)
        forward = [(i, i + 1) for i in range(count - 1)]
        if periodic:
            forward.append((count - 1, 0))
        backward = [(target, source) for source, target in forward]
        low = lax.ppermute(
            lax.slice_in_dim(block, block.shape[dim] - width, None, axis=dim), axis, forward
        )
        high = lax.ppermute(lax.slice_in_dim(block, 0, width, axis=dim), axis, backward)
        block = jnp.concatenate([low, block, high], axis=dim)
    return block


def depthwise(padded, kernel, tile_h, tile_w):
    total = jnp.zeros(padded.shape[:-3] + (tile_h, tile_w, padded.shape[-1]), jnp.float32)
    for row_off in range(7):
        for col_off in range(7):
            total = (
                total
                + padded[..., row_off : row_off + tile_h, col_off : col_off + tile_w, :]
                * kernel[row_off, col_off]
            )
    return total


def depthwise_back(padded, kernel, tile_h, tile_w):
    total = jnp.zeros(padded.shape[:-3] + (tile_h, tile_w, padded.shape[-1]), jnp.float32)
    for row_off in range(7):
        for col_off in range(7):
            total = (
                total
                + padded[
                    ..., 6 - row_off : 6 - row_off + tile_h, 6 - col_off : 6 - col_off + tile_w, :
                ]
                * kernel[row_off, col_off]
            )
    return total


def kernel_grad(grad, padded, tile_h, tile_w):
    lead = tuple(range(grad.ndim - 1))
    return jnp.stack(
        [
            jnp.stack(
                [
                    jnp.sum(
                        grad
                        * padded[..., row_off : row_off + tile_h, col_off : col_off + tile_w, :],
                        axis=lead,
                    )
                    for col_off in range(7)
                ]
            )
            for row_off in range(7)
        ]
    )


def gelu_tanh(values):
    return jax.nn.gelu(values, approximate=True)


def mlp_pass(act_rows, out_grad, w_in, b_in, w_out, b_out, layer_scale):
    pre = jnp.dot(act_rows, w_in, preferred_element_type=jnp.float32) + b_in
    hidden, gelu_back = jax.vjp(gelu_tanh, pre)
    hidden_b = hidden.astype(jnp.bfloat16)
    branch = jnp.dot(hidden_b, w_out, preferred_element_type=jnp.float32) + b_out
    branch_grad = out_grad * layer_scale
    branch_b = branch_grad.astype(jnp.bfloat16)
    hidden_grad = jnp.dot(branch_b, w_out.T, preferred_element_type=jnp.float32)
    pre_grad = gelu_back(hidden_grad)[0]
    pre_b = pre_grad.astype(jnp.bfloat16)
    act_grad = jnp.dot(pre_b, w_in.T, preferred_element_type=jnp.float32)
    grads = (
        jnp.dot(act_rows.T, pre_b, preferred_element_type=jnp.float32),
        jnp.sum(pre_grad, axis=0),
        jnp.dot(hidden_b.T, branch_b, preferred_element_type=jnp.float32),
        jnp.sum(branch_grad, axis=0),
        jnp.sum(out_grad * branch, axis=0),
    )
    return (branch, act_grad, grads)


def body(
    fields,
    cotangent,
    ocean_mask,
    dw_kernel,
    dw_bias,
    ln_gain,
    ln_bias,
    w_in,
    b_in,
    w_out,
    b_out,
    layer_scale,
):
    snapshots, tile_h, tile_w, channels = fields.shape
    cells = tile_h * tile_w
    ocean = ocean_mask.astype(jnp.float32)[None, :, :, None]
    start_b = fields * ocean_mask.astype(jnp.bfloat16)[None, :, :, None]
    lat_ext = padded_2(start_b, (("lat", 1),), 3, False)
    padded = padded_2(lat_ext, (("lon", 2),), 3, True).astype(jnp.float32)
    start = start_b.astype(jnp.float32)
    conv_out = depthwise(padded, dw_kernel, tile_h, tile_w) + dw_bias
    center = jnp.mean(conv_out, axis=-1, keepdims=True)
    shifted = conv_out - center
    inv_std = lax.rsqrt(jnp.mean(shifted * shifted, axis=-1, keepdims=True) + EPS)
    normed = shifted * inv_std
    act = (normed * ln_gain + ln_bias).astype(jnp.bfloat16)
    out_grad = cotangent.astype(jnp.float32) * ocean
    flat_branch, flat_act_grad, mlp_sums = mlp_pass(
        act.reshape(-1, channels),
        out_grad.reshape(-1, channels),
        w_in,
        b_in,
        w_out,
        b_out,
        layer_scale,
    )
    branch = flat_branch.reshape(fields.shape)
    act_grad = flat_act_grad.reshape(fields.shape)
    block_out = (ocean * (start + layer_scale * branch)).astype(jnp.bfloat16)
    scaled = act_grad * ln_gain
    conv_grad = inv_std * (
        scaled
        - jnp.mean(scaled, axis=-1, keepdims=True)
        - normed * jnp.mean(scaled * normed, axis=-1, keepdims=True)
    )
    grad_lat = padded_2(conv_grad.astype(jnp.bfloat16), (("lat", 1),), 3, False).astype(
        conv_grad.dtype
    )
    grad_padded = padded_2(grad_lat.astype(jnp.bfloat16), (("lon", 2),), 3, True).astype(
        grad_lat.dtype
    )
    field_grad = (
        ocean * (out_grad + depthwise_back(grad_padded, dw_kernel, tile_h, tile_w))
    ).astype(jnp.bfloat16)
    lead = (0, 1, 2)
    local = (
        kernel_grad(conv_grad, padded, tile_h, tile_w),
        jnp.sum(conv_grad, axis=lead),
        jnp.sum(act_grad * normed, axis=lead),
        jnp.sum(act_grad, axis=lead),
    ) + mlp_sums
    members = lax.axis_size("lon") * lax.axis_size("lat") * lax.axis_size("dp")
    factor = 1.0 / math.sqrt(snapshots * cells * members)
    summed = lax.psum(
        (local[0], local[1], local[2], local[3], local[4], local[5], local[6], local[7], local[8]),
        ("lon", "lat", "dp"),
    )
    finals = [piece * factor for piece in summed]
    return (
        block_out,
        field_grad,
        finals[0],
        finals[1],
        finals[2],
        finals[3],
        finals[4],
        finals[5],
        finals[6],
        finals[7],
        finals[8],
    )


def solution(mesh):
    return jax.shard_map(
        body,
        mesh=mesh,
        in_specs=(
            P(("groups", "dp"), "lat", "lon", None),
            P(("groups", "dp"), "lat", "lon", None),
            P("lat", "lon"),
            P(),
            P(),
            P(),
            P(),
            P(),
            P(),
            P(),
            P(),
            P(),
        ),
        out_specs=(
            P(("groups", "dp"), "lat", "lon", None),
            P(("groups", "dp"), "lat", "lon", None),
            P("groups", None, None),
            P("groups"),
            P("groups"),
            P("groups"),
            P("groups", None),
            P("groups"),
            P("groups", None),
            P("groups"),
            P("groups"),
        ),
        check_vma=False,
    )
```

profile of v0, /device:TPU:0, one launch (start us, length us, event | category | flops | bytes accessed | tf_op | source)
XLA Modules:
  0.0 214.5 jit_solution(16185889891956108017)
XLA Ops:
  7.2 0.8 fusion.69
  8.0 1.0 broadcast_multiply_fusion.2
  9.0 4.9 %collective-permute-start = (bf16[1,3,16,192]{3,2,1,0:T(8,128)(2,1)S(1)}, bf16[1,3,16,192]{3,2,1,0:T(8,128)(2,1)S(1)}, u32[]{:S(2)}, u32[]{:S(2)}) collective-permute-start(bf16[1,3,16,192]{3,2,1,0:T(8,128)(2,1)S(1)} %get-tuple-element.86), channel_id=1, source_target_pairs={{0,2},{1,3},{4,6},{5,7},{8,10},{9,11},{12,14},{13,15},{16,18},{17,... | collective-permute-start | bytes 55304 | tf_op jit(solution)/shard_map/ppermute | solution.py:18
  13.9 1.3 collective-permute-start.1
  15.6 4.1 %collective-permute-done.1 = bf16[1,3,16,192]{3,2,1,0:T(8,128)(2,1)S(1)} collective-permute-done((bf16[1,3,16,192]{3,2,1,0:T(8,128)(2,1)S(1)}, bf16[1,3,16,192]{3,2,1,0:T(8,128)(2,1)S(1)}, u32[]{:S(2)}, u32[]{:S(2)}) %collective-permute-start.1) | collective-permute-done | bytes 18464 | tf_op jit(solution)/shard_map/ppermute | solution.py:21
  19.7 1.6 collective-permute-start.2
  21.3 2.2 %collective-permute-start.3 = (bf16[1,22,3,192]{3,2,1,0:T(4,128)(2,1)S(1)}, bf16[1,22,3,192]{3,2,1,0:T(4,128)(2,1)S(1)}, u32[]{:S(2)}, u32[]{:S(2)}) collective-permute-start(bf16[1,22,3,192]{3,2,1,0:T(4,128)(2,1)S(1)} %get-tuple-element.81), channel_id=1, source_target_pairs={{4,0},{8,4},{12,8},{0,12},{5,1},{9,5},{13,9},{1,13},{6,2},{10,6},{... | collective-permute-start | bytes 76040 | tf_op jit(solution)/shard_map/ppermute | solution.py:21
  23.6 0.6 fusion.68
  24.2 1.5 collective-permute-done.2
  25.7 0.2 collective-permute-done.3
  26.4 0.3 copy-done.90
  26.7 2.4 %fusion.63 = (f32[16,16]{1,0:T(8,128)S(1)}, f32[1,16,16,192]{3,2,1,0:T(8,128)S(1)}) fusion(f32[192]{0:T(256)S(1)} %copy-done.90, f32[192]{0:T(256)S(1)} %bitcast.228, f32[1,22,22,192]{3,2,1,0:T(8,128)S(1)} %maximum_convert_fusion, f32[192]{0:T(256)} %bitcast.47, f32[192]{0:T(256)S(1)} %bitcast.136, f32[192]{0:T(256)S(1)} %bitcast.138, f32[192]{0:T(256)S(1)} %bitcast.140, ...), kind=kLoop, calls=%fused_computation.208 | loop fusion | flops 4865792 | bytes 9869824 | tf_op jit(solution)/shard_map/reduce_sum | solution.py:118
  29.1 0.2 multiply_reduce_fusion.52
  29.4 0.1 add_convert_fusion
  29.5 0.6 copy-done.1
  30.1 0.2 convolution_add_fusion
  30.3 0.4 copy-done.94
  30.8 0.4 convolution_add_fusion.1
  31.2 0.1 copy.27
  31.3 0.7 copy-done.3
  32.1 1.4 multiply_reduce_fusion
  33.5 1.3 fusion.70
  34.8 1.0 fusion.62
  35.7 0.1 copy.28
  35.9 0.2 multiply_reduce_fusion.1
  36.2 0.7 multiply_reduce_fusion.2
  36.9 0.6 multiply_reduce_fusion.20
  37.5 0.4 multiply_reduce_fusion.38
  38.0 0.6 copy-done.93
  38.6 1.2 fusion.61
  39.8 1.1 fusion.57
  41.3 0.5 copy-done.89
  41.8 0.2 copy-done.88
  42.0 58.4 %all-reduce = (f32[7,7,192]{2,1,0:T(8,128)S(1)}, f32[192]{0:T(256)S(1)}, f32[192]{0:T(256)S(1)}, f32[192]{0:T(256)S(1)}, f32[768]{0:T(1024)S(1)}, /*index=5*/f32[192]{0:T(256)S(1)}, f32[192]{0:T(256)S(1)}) all-reduce(f32[7,7,192]{2,1,0:T(8,128)S(1)} %constant_dynamic-update-s, ...), channel_id=1, replica_groups=mesh['groups'=2,'lon'=4,'lat'=2,'dp'=2] {'lon','lat','dp'}, use_global_device_ids=true, to_apply=%region_53.0 | all-reduce | flops 11136 | bytes 89088 | tf_op jit(solution)/shard_map/psum | solution.py:160
  100.4 0.6 broadcast_multiply_fusion.3
  101.0 0.6 broadcast_multiply_fusion.6
  101.6 1.3 collective-permute-start.4
  102.9 1.3 collective-permute-start.5
  104.2 0.6 broadcast_multiply_fusion.7
  104.8 0.6 broadcast_multiply_fusion.9
  105.3 3.3 %collective-permute-done.5 = bf16[1,3,16,192]{3,2,1,0:T(8,128)(2,1)S(1)} collective-permute-done((bf16[1,3,16,192]{3,2,1,0:T(8,128)(2,1)S(1)}, bf16[1,3,16,192]{3,2,1,0:T(8,128)(2,1)S(1)}, u32[]{:S(2)}, u32[]{:S(2)}) %collective-permute-start.5) | collective-permute-done | bytes 18464 | tf_op jit(solution)/shard_map/ppermute | solution.py:21
  108.7 3.8 %collective-permute-start.7 = (bf16[1,22,3,192]{3,2,1,0:T(4,128)(2,1)S(1)}, bf16[1,22,3,192]{3,2,1,0:T(4,128)(2,1)S(1)}, u32[]{:S(2)}, u32[]{:S(2)}) collective-permute-start(bf16[1,22,3,192]{3,2,1,0:T(4,128)(2,1)S(1)} %get-tuple-element.79), channel_id=1, source_target_pairs={{4,0},{8,4},{12,8},{0,12},{5,1},{9,5},{13,9},{1,13},{6,2},{10,6},{... | collective-permute-start | bytes 76040 | tf_op jit(solution)/shard_map/ppermute | solution.py:21
  112.5 0.6 broadcast_multiply_fusion.11
  113.5 1.0 collective-permute-done.6
  115.1 3.3 %fusion.9 = bf16[1,16,16,192]{3,2,1,0:T(8,128)(2,1)} fusion(f32[1,22,22,192]{3,2,1,0:T(8,128)S(1)} %maximum_convert_fusion.1, f32[192]{0:T(256)S(1)} %bitcast.229, f32[192]{0:T(256)} %bitcast.47, f32[192]{0:T(256)S(1)} %bitcast.137, f32[192]{0:T(256)S(1)} %bitcast.139, f32[192]{0:T(256)S(1)} %bitcast.141, f32[192]{0:T(256)S(1)} %bitcast.143, ...), kind=kLoop, calls=%fused_computation.19 | loop fusion | flops 5013504 | bytes 9869056 | tf_op jit(solution)/shard_map/convert_element_type | solution.py:150
  118.4 86.5 %all-reduce.4.cloned.1.call-done = (f32[192,768]{1,0:T(8,128)}, f32[768,192]{0,1:T(8,128)}) async-done(((f32[192,768]{1,0:T(8,128)}, f32[768,192]{0,1:T(8,128)}), (f32[192,768]{1,0:T(8,128)}, f32[768,192]{0,1:T(8,128)})) %all-reduce.4.cloned.1.call-update) | async-done | bytes 1179664 | tf_op jit(solution)/shard_map/psum | solution.py:160
  204.8 2.0 broadcast_multiply_fusion
  206.8 0.9 broadcast_multiply_fusion.1
  (218 shorter events, 1.5 us)
Async XLA Ops:
  7.2 23.2 %copy-start = (bf16[768,192]{0,1:T(8,128)(2,1)S(1)}, bf16[768,192]{0,1:T(8,128)(2,1)}, u32[]{:S(2)}) copy-start(bf16[768,192]{0,1:T(8,128)(2,1)} %param.21) | copy-start | bytes 884740
  7.2 197.7 %all-reduce.4.cloned.1.call-start = ((), (), s32[]{:S(2)}) async-start(), calls=%async_computation | async-start | bytes 2359296 | tf_op jit(solution)/shard_map/psum | solution.py:160
  9.0 6.2 %copy-start.6 = (f32[7,7,192]{2,1,0:T(8,128)S(1)}, f32[7,7,192]{2,1,0:T(8,128)}, u32[]{:S(2)}) copy-start(f32[7,7,192]{2,1,0:T(8,128)} %param.15) | copy-start | bytes 112900
  9.0 6.5 %collective-permute-start = (bf16[1,3,16,192]{3,2,1,0:T(8,128)(2,1)S(1)}, bf16[1,3,16,192]{3,2,1,0:T(8,128)(2,1)S(1)}, u32[]{:S(2)}, u32[]{:S(2)}) collective-permute-start(bf16[1,3,16,192]{3,2,1,0:T(8,128)(2,1)S(1)} %get-tuple-element.86), channel_id=1, source_target_pairs={{0,2},{1,3},{4,6},{5,7},{8,10},{9,11},{12,14},{13,15},{16,18},{17,... | collective-permute-start | bytes 55304 | tf_op jit(solution)/shard_map/ppermute | solution.py:18
  13.9 5.7 %collective-permute-start.1 = (bf16[1,3,16,192]{3,2,1,0:T(8,128)(2,1)S(1)}, bf16[1,3,16,192]{3,2,1,0:T(8,128)(2,1)S(1)}, u32[]{:S(2)}, u32[]{:S(2)}) collective-permute-start(bf16[1,3,16,192]{3,2,1,0:T(8,128)(2,1)S(1)} %get-tuple-element.87), channel_id=1, source_target_pairs={{2,0},{3,1},{6,4},{7,5},{10,8},{11,9},{14,12},{15,13},{18,16},{19,... | collective-permute-start | bytes 55304 | tf_op jit(solution)/shard_map/ppermute | solution.py:21
  15.3 10.7 %copy-start.8 = (f32[1,1,192]{2,1,0:T(1,128)}, f32[1,1,192]{2,1,0:T(1,128)S(1)}, u32[]{:S(2)}) copy-start(f32[1,1,192]{2,1,0:T(1,128)S(1)} %get-tuple-element.97) | copy-start | bytes 2308
  15.3 10.7 %copy-start.10 = (f32[1,1,192]{2,1,0:T(1,128)}, f32[1,1,192]{2,1,0:T(1,128)S(1)}, u32[]{:S(2)}) copy-start(f32[1,1,192]{2,1,0:T(1,128)S(1)} %get-tuple-element.98) | copy-start | bytes 2308
  15.3 10.7 %copy-start.12 = (f32[1,1,192]{2,1,0:T(1,128)}, f32[1,1,192]{2,1,0:T(1,128)S(1)}, u32[]{:S(2)}) copy-start(f32[1,1,192]{2,1,0:T(1,128)S(1)} %get-tuple-element.99) | copy-start | bytes 2308
  15.3 10.7 %copy-start.14 = (f32[1,1,192]{2,1,0:T(1,128)}, f32[1,1,192]{2,1,0:T(1,128)S(1)}, u32[]{:S(2)}) copy-start(f32[1,1,192]{2,1,0:T(1,128)S(1)} %get-tuple-element.100) | copy-start | bytes 2308
  15.3 10.7 %copy-start.16 = (f32[1,1,192]{2,1,0:T(1,128)}, f32[1,1,192]{2,1,0:T(1,128)S(1)}, u32[]{:S(2)}) copy-start(f32[1,1,192]{2,1,0:T(1,128)S(1)} %get-tuple-element.101) | copy-start | bytes 2308
  15.3 10.7 %copy-start.18 = (f32[1,1,192]{2,1,0:T(1,128)}, f32[1,1,192]{2,1,0:T(1,128)S(1)}, u32[]{:S(2)}) copy-start(f32[1,1,192]{2,1,0:T(1,128)S(1)} %get-tuple-element.102) | copy-start | bytes 2308
  15.3 10.7 %copy-start.20 = (f32[1,1,192]{2,1,0:T(1,128)}, f32[1,1,192]{2,1,0:T(1,128)S(1)}, u32[]{:S(2)}) copy-start(f32[1,1,192]{2,1,0:T(1,128)S(1)} %get-tuple-element.103) | copy-start | bytes 2308
  15.3 10.7 %copy-start.22 = (f32[1,1,192]{2,1,0:T(1,128)}, f32[1,1,192]{2,1,0:T(1,128)S(1)}, u32[]{:S(2)}) copy-start(f32[1,1,192]{2,1,0:T(1,128)S(1)} %get-tuple-element.104) | copy-start | bytes 2308
  15.3 10.7 %copy-start.24 = (f32[1,1,192]{2,1,0:T(1,128)}, f32[1,1,192]{2,1,0:T(1,128)S(1)}, u32[]{:S(2)}) copy-start(f32[1,1,192]{2,1,0:T(1,128)S(1)} %get-tuple-element.105) | copy-start | bytes 2308
  15.4 10.7 %copy-start.26 = (f32[1,1,192]{2,1,0:T(1,128)}, f32[1,1,192]{2,1,0:T(1,128)S(1)}, u32[]{:S(2)}) copy-start(f32[1,1,192]{2,1,0:T(1,128)S(1)} %get-tuple-element.106) | copy-start | bytes 2308
  15.4 10.7 %copy-start.28 = (f32[1,1,192]{2,1,0:T(1,128)}, f32[1,1,192]{2,1,0:T(1,128)S(1)}, u32[]{:S(2)}) copy-start(f32[1,1,192]{2,1,0:T(1,128)S(1)} %get-tuple-element.107) | copy-start | bytes 2308
  15.4 10.7 %copy-start.30 = (f32[1,1,192]{2,1,0:T(1,128)}, f32[1,1,192]{2,1,0:T(1,128)S(1)}, u32[]{:S(2)}) copy-start(f32[1,1,192]{2,1,0:T(1,128)S(1)} %get-tuple-element.108) | copy-start | bytes 2308
  15.4 10.7 %copy-start.32 = (f32[1,1,192]{2,1,0:T(1,128)}, f32[1,1,192]{2,1,0:T(1,128)S(1)}, u32[]{:S(2)}) copy-start(f32[1,1,192]{2,1,0:T(1,128)S(1)} %get-tuple-element.109) | copy-start | bytes 2308
  15.4 10.7 %copy-start.34 = (f32[1,1,192]{2,1,0:T(1,128)}, f32[1,1,192]{2,1,0:T(1,128)S(1)}, u32[]{:S(2)}) copy-start(f32[1,1,192]{2,1,0:T(1,128)S(1)} %get-tuple-element.110) | copy-start | bytes 2308
  15.4 10.7 %copy-start.36 = (f32[1,1,192]{2,1,0:T(1,128)}, f32[1,1,192]{2,1,0:T(1,128)S(1)}, u32[]{:S(2)}) copy-start(f32[1,1,192]{2,1,0:T(1,128)S(1)} %get-tuple-element.111) | copy-start | bytes 2308
  15.4 10.7 %copy-start.38 = (f32[1,1,192]{2,1,0:T(1,128)}, f32[1,1,192]{2,1,0:T(1,128)S(1)}, u32[]{:S(2)}) copy-start(f32[1,1,192]{2,1,0:T(1,128)S(1)} %get-tuple-element.112) | copy-start | bytes 2308
  15.5 10.7 %copy-start.40 = (f32[1,1,192]{2,1,0:T(1,128)}, f32[1,1,192]{2,1,0:T(1,128)S(1)}, u32[]{:S(2)}) copy-start(f32[1,1,192]{2,1,0:T(1,128)S(1)} %get-tuple-element.113) | copy-start | bytes 2308
  15.5 10.7 %copy-start.42 = (f32[1,1,192]{2,1,0:T(1,128)}, f32[1,1,192]{2,1,0:T(1,128)S(1)}, u32[]{:S(2)}) copy-start(f32[1,1,192]{2,1,0:T(1,128)S(1)} %get-tuple-element.114) | copy-start | bytes 2308
  15.5 10.7 %copy-start.44 = (f32[1,1,192]{2,1,0:T(1,128)}, f32[1,1,192]{2,1,0:T(1,128)S(1)}, u32[]{:S(2)}) copy-start(f32[1,1,192]{2,1,0:T(1,128)S(1)} %get-tuple-element.115) | copy-start | bytes 2308
  15.5 10.7 %copy-start.46 = (f32[1,1,192]{2,1,0:T(1,128)}, f32[1,1,192]{2,1,0:T(1,128)S(1)}, u32[]{:S(2)}) copy-start(f32[1,1,192]{2,1,0:T(1,128)S(1)} %get-tuple-element.116) | copy-start | bytes 2308
  15.5 10.7 %copy-start.48 = (f32[1,1,192]{2,1,0:T(1,128)}, f32[1,1,192]{2,1,0:T(1,128)S(1)}, u32[]{:S(2)}) copy-start(f32[1,1,192]{2,1,0:T(1,128)S(1)} %get-tuple-element.117) | copy-start | bytes 2308
  15.5 10.7 %copy-start.50 = (f32[1,1,192]{2,1,0:T(1,128)}, f32[1,1,192]{2,1,0:T(1,128)S(1)}, u32[]{:S(2)}) copy-start(f32[1,1,192]{2,1,0:T(1,128)S(1)} %get-tuple-element.118) | copy-start | bytes 2308
  15.5 10.7 %copy-start.52 = (f32[1,1,192]{2,1,0:T(1,128)}, f32[1,1,192]{2,1,0:T(1,128)S(1)}, u32[]{:S(2)}) copy-start(f32[1,1,192]{2,1,0:T(1,128)S(1)} %get-tuple-element.119) | copy-start | bytes 2308
  15.5 10.7 %copy-start.54 = (f32[1,1,192]{2,1,0:T(1,128)}, f32[1,1,192]{2,1,0:T(1,128)S(1)}, u32[]{:S(2)}) copy-start(f32[1,1,192]{2,1,0:T(1,128)S(1)} %get-tuple-element.120) | copy-start | bytes 2308
  15.5 10.7 %copy-start.56 = (f32[1,1,192]{2,1,0:T(1,128)}, f32[1,1,192]{2,1,0:T(1,128)S(1)}, u32[]{:S(2)}) copy-start(f32[1,1,192]{2,1,0:T(1,128)S(1)} %get-tuple-element.121) | copy-start | bytes 2308
  15.5 10.7 %copy-start.58 = (f32[1,1,192]{2,1,0:T(1,128)}, f32[1,1,192]{2,1,0:T(1,128)S(1)}, u32[]{:S(2)}) copy-start(f32[1,1,192]{2,1,0:T(1,128)S(1)} %get-tuple-element.122) | copy-start | bytes 2308
  15.6 10.7 %copy-start.60 = (f32[1,1,192]{2,1,0:T(1,128)}, f32[1,1,192]{2,1,0:T(1,128)S(1)}, u32[]{:S(2)}) copy-start(f32[1,1,192]{2,1,0:T(1,128)S(1)} %get-tuple-element.123) | copy-start | bytes 2308
  15.6 10.7 %copy-start.62 = (f32[1,1,192]{2,1,0:T(1,128)}, f32[1,1,192]{2,1,0:T(1,128)S(1)}, u32[]{:S(2)}) copy-start(f32[1,1,192]{2,1,0:T(1,128)S(1)} %get-tuple-element.124) | copy-start | bytes 2308
  15.6 10.7 %copy-start.64 = (f32[1,1,192]{2,1,0:T(1,128)}, f32[1,1,192]{2,1,0:T(1,128)S(1)}, u32[]{:S(2)}) copy-start(f32[1,1,192]{2,1,0:T(1,128)S(1)} %get-tuple-element.125) | copy-start | bytes 2308
  19.7 6.0 %collective-permute-start.2 = (bf16[1,22,3,192]{3,2,1,0:T(4,128)(2,1)S(1)}, bf16[1,22,3,192]{3,2,1,0:T(4,128)(2,1)S(1)}, u32[]{:S(2)}, u32[]{:S(2)}) collective-permute-start(bf16[1,22,3,192]{3,2,1,0:T(4,128)(2,1)S(1)} %get-tuple-element.80), channel_id=1, source_target_pairs={{0,4},{4,8},{8,12},{12,0},{1,5},{5,9},{9,13},{13,1},{2,6},{6,10},{... | collective-permute-start | bytes 76040 | tf_op jit(solution)/shard_map/ppermute | solution.py:18
  21.3 4.5 %collective-permute-start.3 = (bf16[1,22,3,192]{3,2,1,0:T(4,128)(2,1)S(1)}, bf16[1,22,3,192]{3,2,1,0:T(4,128)(2,1)S(1)}, u32[]{:S(2)}, u32[]{:S(2)}) collective-permute-start(bf16[1,22,3,192]{3,2,1,0:T(4,128)(2,1)S(1)} %get-tuple-element.81), channel_id=1, source_target_pairs={{4,0},{8,4},{12,8},{0,12},{5,1},{9,5},{13,9},{1,13},{6,2},{10,6},{... | collective-permute-start | bytes 76040 | tf_op jit(solution)/shard_map/ppermute | solution.py:21
  24.2 2.1 %copy-start.74 = (f32[1,1,192]{2,1,0:T(1,128)}, f32[1,1,192]{2,1,0:T(1,128)S(1)}, u32[]{:S(2)}) copy-start(f32[1,1,192]{2,1,0:T(1,128)S(1)} %get-tuple-element.130) | copy-start | bytes 2308
  24.2 2.1 %copy-start.76 = (f32[1,1,192]{2,1,0:T(1,128)}, f32[1,1,192]{2,1,0:T(1,128)S(1)}, u32[]{:S(2)}) copy-start(f32[1,1,192]{2,1,0:T(1,128)S(1)} %get-tuple-element.131) | copy-start | bytes 2308
  24.2 2.1 %copy-start.78 = (f32[1,1,192]{2,1,0:T(1,128)}, f32[1,1,192]{2,1,0:T(1,128)S(1)}, u32[]{:S(2)}) copy-start(f32[1,1,192]{2,1,0:T(1,128)S(1)} %get-tuple-element.132) | copy-start | bytes 2308
  24.2 2.1 %copy-start.80 = (f32[1,1,192]{2,1,0:T(1,128)}, f32[1,1,192]{2,1,0:T(1,128)S(1)}, u32[]{:S(2)}) copy-start(f32[1,1,192]{2,1,0:T(1,128)S(1)} %get-tuple-element.133) | copy-start | bytes 2308
  24.2 2.1 %copy-start.82 = (f32[1,1,192]{2,1,0:T(1,128)}, f32[1,1,192]{2,1,0:T(1,128)S(1)}, u32[]{:S(2)}) copy-start(f32[1,1,192]{2,1,0:T(1,128)S(1)} %get-tuple-element.134) | copy-start | bytes 2308
  24.2 2.1 %copy-start.84 = (f32[1,1,192]{2,1,0:T(1,128)}, f32[1,1,192]{2,1,0:T(1,128)S(1)}, u32[]{:S(2)}) copy-start(f32[1,1,192]{2,1,0:T(1,128)S(1)} %get-tuple-element.135) | copy-start | bytes 2308
  26.7 2.7 %copy-start.7 = (f32[192]{0:T(256)S(1)}, f32[192]{0:T(256)}, u32[]{:S(2)}) copy-start(f32[192]{0:T(256)} %param.17) | copy-start | bytes 2308
  26.7 2.7 %copy-start.91 = (f32[192]{0:T(256)S(1)}, f32[192]{0:T(256)}, u32[]{:S(2)}) copy-start(f32[192]{0:T(256)} %param.18) | copy-start | bytes 2308
  101.6 3.7 %collective-permute-start.4 = (bf16[1,3,16,192]{3,2,1,0:T(8,128)(2,1)S(1)}, bf16[1,3,16,192]{3,2,1,0:T(8,128)(2,1)S(1)}, u32[]{:S(2)}, u32[]{:S(2)}) collective-permute-start(bf16[1,3,16,192]{3,2,1,0:T(8,128)(2,1)S(1)} %get-tuple-element.84), channel_id=1, source_target_pairs={{0,2},{1,3},{4,6},{5,7},{8,10},{9,11},{12,14},{13,15},{16,18},{17,... | collective-permute-start | bytes 55304 | tf_op jit(solution)/shard_map/ppermute | solution.py:18
  102.9 5.7 %collective-permute-start.5 = (bf16[1,3,16,192]{3,2,1,0:T(8,128)(2,1)S(1)}, bf16[1,3,16,192]{3,2,1,0:T(8,128)(2,1)S(1)}, u32[]{:S(2)}, u32[]{:S(2)}) collective-permute-start(bf16[1,3,16,192]{3,2,1,0:T(8,128)(2,1)S(1)} %get-tuple-element.85), channel_id=1, source_target_pairs={{2,0},{3,1},{6,4},{7,5},{10,8},{11,9},{14,12},{15,13},{18,16},{19,... | collective-permute-start | bytes 55304 | tf_op jit(solution)/shard_map/ppermute | solution.py:21
  108.7 5.9 %collective-permute-start.6 = (bf16[1,22,3,192]{3,2,1,0:T(4,128)(2,1)S(1)}, bf16[1,22,3,192]{3,2,1,0:T(4,128)(2,1)S(1)}, u32[]{:S(2)}, u32[]{:S(2)}) collective-permute-start(bf16[1,22,3,192]{3,2,1,0:T(4,128)(2,1)S(1)} %get-tuple-element.78), channel_id=1, source_target_pairs={{0,4},{4,8},{8,12},{12,0},{1,5},{5,9},{9,13},{13,1},{2,6},{6,10},{... | collective-permute-start | bytes 76040 | tf_op jit(solution)/shard_map/ppermute | solution.py:18
  108.7 5.8 %collective-permute-start.7 = (bf16[1,22,3,192]{3,2,1,0:T(4,128)(2,1)S(1)}, bf16[1,22,3,192]{3,2,1,0:T(4,128)(2,1)S(1)}, u32[]{:S(2)}, u32[]{:S(2)}) collective-permute-start(bf16[1,22,3,192]{3,2,1,0:T(4,128)(2,1)S(1)} %get-tuple-element.79), channel_id=1, source_target_pairs={{4,0},{8,4},{12,8},{0,12},{5,1},{9,5},{13,9},{1,13},{6,2},{10,6},{... | collective-permute-start | bytes 76040 | tf_op jit(solution)/shard_map/ppermute | solution.py:21
  (56 other events, 81.0 us)
Sparse Core Ops, SparseCore 0:
  113.2 91.5 all-reduce.3
where the time goes:
time: 215 us
  waiting for transfers between devices  96.5 us (45%)
  blocking collectives  58.4 us (27%)
  other arithmetic  17.3 us (8%)
  starting transfers between devices  16.5 us (8%)
  between operations  15.6 us (7%)
  matrix products  5.21 us (2%)
  local copies, waits for them, and re-layouts  5 us (2%)
    psum x1, waiting for transfers between devices, body(): lax.psum((local[0], local[1], local[2], local[3], local[4], local[5], loc...  86.5 us
    psum x1, blocking collectives, body(): lax.psum((local[0], local[1], local[2], local[3], local[4], local[5], loc...  58.4 us
    ppermute x4, starting transfers between devices, padded_2(): lax.ppermute(lax.slice_in_dim(block, 0, width, axis=dim), axis, backward)  8.64 us
    ppermute x4, starting transfers between devices, padded_2(): lax.ppermute(lax.slice_in_dim(block, block.shape[dim] - width, None, axis...  7.84 us
    ppermute x4, waiting for transfers between devices, padded_2(): lax.ppermute(lax.slice_in_dim(block, 0, width, axis=dim), axis, backward)  7.5 us
    mul x7, other arithmetic, body(): finals = [piece * factor for piece in summed]  5.76 us
  transfers between devices with their start and end apart: 9, of which 6 were waited for; matrix products, arithmetic and copies ran while one was open for 3% of the time, Pallas kernels for 0%

commit v1 on v0

--- a/solution.py
+++ b/solution.py
@@ -11,6 +11,9 @@
 def padded_2(block, sides, width, periodic):
     for axis, dim in sides:
         count = lax.axis_size(axis)
+        if count == 2 and not periodic:
+            block = padded_pair(block, axis, dim, width)
+            continue
         forward = [(i, i + 1) for i in range(count - 1)]
         if periodic:
             forward.append((count - 1, 0))
@@ -21,6 +24,95 @@
         high = lax.ppermute(lax.slice_in_dim(block, 0, width, axis=dim), axis, backward)
         block = jnp.concatenate([low, block, high], axis=dim)
     return block
+
+
+def padded_pair(block, axis, dim, width):
+    first = lax.axis_index(axis) == 0
+    head = lax.slice_in_dim(block, 0, width, axis=dim)
+    tail = lax.slice_in_dim(block, block.shape[dim] - width, None, axis=dim)
+    other = lax.ppermute(jnp.where(first, tail, head), axis, [(0, 1), (1, 0)])
+    none = jnp.zeros_like(other)
+    return jnp.concatenate(
+        [jnp.where(first, none, other), block, jnp.where(first, other, none)], axis=dim
+    )
+
+
+LANES = 256
+LINK = jnp.bfloat16
+
+
+def to_rows(piece):
+    rows, columns = piece.shape
+    blocks = -(-columns // LANES)
+    piece = jnp.pad(piece, ((0, 0), (0, blocks * LANES - columns)))
+    return [piece[:, b * LANES : (b + 1) * LANES] for b in range(blocks)]
+
+
+def from_rows(rows_array, start, rows, columns):
+    blocks = -(-columns // LANES)
+    parts = [rows_array[start + b * rows : start + (b + 1) * rows] for b in range(blocks)]
+    return jnp.concatenate(parts, axis=1)[:, :columns], start + blocks * rows
+
+
+def rounds_of(count):
+    if count & (count - 1) == 0 and count <= 4:
+        return [([(i, i ^ step) for i in range(count)], lambda me, s=step: (me ^ s, me ^ s)) for step in range(1, count)]
+    return [
+        (
+            [(i, (i + step) % count) for i in range(count)],
+            lambda me, s=step: (lax.rem(me + s, count), lax.rem(me + count - s, count)),
+        )
+        for step in range(1, count)
+    ]
+
+
+def scatter_sum(rows_array, axis):
+    count = lax.axis_size(axis)
+    size = rows_array.shape[0] // count
+    me = lax.axis_index(axis)
+    total = lax.dynamic_slice_in_dim(rows_array, me * size, size, axis=0)
+    arrived = []
+    for perm, ends in rounds_of(count):
+        target, _ = ends(me)
+        piece = lax.dynamic_slice_in_dim(rows_array, target * size, size, axis=0)
+        arrived.append(lax.ppermute(piece.astype(LINK), axis, perm))
+    for piece in arrived:
+        total = total + piece.astype(jnp.float32)
+    return total
+
+
+def gather_rows(piece, axis):
+    count = lax.axis_size(axis)
+    size = piece.shape[0]
+    me = lax.axis_index(axis)
+    whole = jnp.zeros((count * size,) + piece.shape[1:], piece.dtype)
+    whole = lax.dynamic_update_slice_in_dim(whole, piece, me * size, axis=0)
+    for perm, ends in rounds_of(count):
+        _, source = ends(me)
+        other = lax.ppermute(piece, axis, perm)
+        whole = lax.dynamic_update_slice_in_dim(whole, other, source * size, axis=0)
+    return whole
+
+
+def sum_over(pieces, axes, factor):
+    members = math.prod(lax.axis_size(axis) for axis in axes)
+    stacked = sum((to_rows(piece) for piece in pieces), [])
+    rows = sum(part.shape[0] for part in stacked)
+    quantum = members * 8
+    extra = -rows % quantum
+    stacked.append(jnp.zeros((extra, LANES), jnp.float32))
+    total = jnp.concatenate(stacked, axis=0)
+    for axis in axes:
+        total = scatter_sum(total, axis)
+    total = (total * factor).astype(LINK)
+    for axis in reversed(axes):
+        total = gather_rows(total, axis)
+    total = total.astype(jnp.float32)
+    out, start = [], 0
+    for piece in pieces:
+        value, start = from_rows(total, start, *piece.shape)
+        out.append(value)
+    return out
 
 
 def depthwise(padded, kernel, tile_h, tile_w):
@@ -86,7 +178,7 @@
     grads = (
         jnp.dot(act_rows.T, pre_b, preferred_element_type=jnp.float32),
         jnp.sum(pre_grad, axis=0),
-        jnp.dot(hidden_b.T, branch_b, preferred_element_type=jnp.float32),
+        jnp.dot(branch_b.T, hidden_b, preferred_element_type=jnp.float32),
         jnp.sum(branch_grad, axis=0),
         jnp.sum(out_grad * branch, axis=0),
     )
@@ -157,11 +249,29 @@
     ) + mlp_sums
     members = lax.axis_size("lon") * lax.axis_size("lat") * lax.axis_size("dp")
     factor = 1.0 / math.sqrt(snapshots * cells * members)
-    summed = lax.psum(
-        (local[0], local[1], local[2], local[3], local[4], local[5], local[6], local[7], local[8]),
-        ("lon", "lat", "dp"),
-    )
-    finals = [piece * factor for piece in summed]
+    hid = w_in.shape[1]
+    smalls = jnp.concatenate(
+        [
+            local[0].reshape(-1, channels),
+            jnp.stack([local[1], local[2], local[3], local[7], local[8]]),
+            local[5].reshape(-1, channels),
+        ],
+        axis=0,
+    )
+    got = sum_over([local[4], local[6], smalls], ("dp", "lat", "lon"), factor)
+    taps = dw_kernel.shape[0] * dw_kernel.shape[1]
+    small = got[2]
+    finals = (
+        small[:taps].reshape(dw_kernel.shape),
+        small[taps],
+        small[taps + 1],
+        small[taps + 2],
+        got[0],
+        small[taps + 5 :].reshape(hid),
+        got[1].T,
+        small[taps + 3],
+        small[taps + 4],
+    )
     return (
         block_out,
         field_grad,

time: 215 us -> 71.4 us (0.33)
  waiting for transfers between devices: 96.5 us -> 19.7 us
  blocking collectives: 58.4 us -> 0 us
  between operations: 15.6 us -> 2.47 us
  starting transfers between devices: 16.5 us -> 21.8 us
  local copies, waits for them, and re-layouts: 5 us -> 8.58 us
  other arithmetic: 17.3 us -> 14.1 us
    psum x1 -> x0, waiting for transfers between devices: 86.5 us -> none  [body(): lax.psum((local[0], local[1], local[2], local[3], local[4], local[5], loc...]
    psum x1 -> x0, blocking collectives: 58.4 us -> none  [body(): lax.psum((local[0], local[1], local[2], local[3], local[4], local[5], loc...]
    ppermute x0 -> x12, waiting for transfers between devices: none -> 18.8 us  [the longest x5 9.99 us: scatter_sum(): arrived.append(lax.ppermute(piece.astype(LINK), axis, perm))]
    ppermute x0 -> x12, starting transfers between devices: none -> 14.1 us  [the longest x5 5.94 us: scatter_sum(): arrived.append(lax.ppermute(piece.astype(LINK), axis, perm))]
    ppermute x4 -> x2, waiting for transfers between devices: 7.5 us -> 0.01 us  [padded_2(): lax.ppermute(lax.slice_in_dim(block, 0, width, axis=dim), axis, backward)]
    ppermute x4 -> x2, starting transfers between devices: 7.84 us -> 1.7 us  [padded_2(): lax.ppermute(lax.slice_in_dim(block, block.shape[dim] - width, None, axis...]
    mul x7 -> x0, other arithmetic: 5.76 us -> none  [body(): finals = [piece * factor for piece in summed]]
    unnamed x196 -> x194, local copies, waits for them, and re-layouts: 3.73 us -> 0.86 us
  transfers between devices with their start and end apart: 9 -> 16, of which waited for: 6 -> 9; matrix products, arithmetic and copies ran while one was open for 3% -> 10% of each run, Pallas kernels for 0% -> 0%
where the time goes in v1:
time: 71.4 us; the launch traced here: 71 us
  starting transfers between devices  21.8 us (31%)
  waiting for transfers between devices  19.7 us (28%)
  other arithmetic  14.1 us (20%)
  local copies, waits for them, and re-layouts  8.58 us (12%)
  matrix products  4.41 us (6%)
  between operations  2.47 us (3%)
    ppermute x5, waiting for transfers between devices, scatter_sum(): arrived.append(lax.ppermute(piece.astype(LINK), axis, perm))  9.99 us
    ppermute x5, waiting for transfers between devices, gather_rows(): other = lax.ppermute(piece, axis, perm)  8.82 us
    ppermute x2, starting transfers between devices, padded_2(): lax.ppermute(lax.slice_in_dim(block, 0, width, axis=dim), axis, backward)  6.05 us
    ppermute x5, starting transfers between devices, scatter_sum(): arrived.append(lax.ppermute(piece.astype(LINK), axis, perm))  5.94 us
    ppermute x5, starting transfers between devices, gather_rows(): other = lax.ppermute(piece, axis, perm)  4.41 us
    ppermute x2, starting transfers between devices, padded_pair(): other = lax.ppermute(jnp.where(first, tail, head), axis, [(0, 1), (1, 0)])  3.7 us
    slice x3, local copies, waits for them, and re-layouts, depthwise(): kernel[row_off, col_off]  3.48 us
    convert_element_type x1, other arithmetic, body(): field_grad = (ocean * (out_grad + depthwise_back(grad_padded, dw_kernel,...  3.3 us
  transfers between devices with their start and end apart: 16, of which 9 were waited for; matrix products, arithmetic and copies ran while one was open for 10% of the time, Pallas kernels for 0%

profile of v1, /device:TPU:0, one launch (start us, length us, event | category | flops | bytes accessed | tf_op | source)
XLA Modules:
  0.0 71.0 jit_solution(12286281686166161382)
XLA Ops:
  0.7 0.8 %fusion.71 = (f32[16,16]{1,0:T(8,128)S(1)}, bf16[16,16]{1,0:T(8,128)(2,1)S(1)}) fusion(s32[16,16]{1,0:T(8,128)} %param.14), kind=kLoop, calls=%fused_computation.231 | loop fusion | flops 512 | bytes 2560 | tf_op jit(solution)/shard_map/convert_element_type | solution.py:204
  1.5 1.0 %broadcast_multiply_fusion = bf16[1,16,16,192]{3,2,1,0:T(8,128)(2,1)S(1)} fusion(bf16[1,16,16,192]{3,2,1,0:T(8,128)(2,1)} %param.12, bf16[16,16]{1,0:T(8,128)(2,1)S(1)} %get-tuple-element.152), kind=kLoop, calls=%fused_computation.189 | loop fusion | flops 49152 | bytes 197120 | tf_op jit(solution)/shard_map/mul | solution.py:205
  2.5 3.0 %collective-permute-start = (bf16[1,3,16,192]{3,2,1,0:T(8,128)(2,1)S(1)}, bf16[1,3,16,192]{3,2,1,0:T(8,128)(2,1)S(1)}, u32[]{:S(2)}, u32[]{:S(2)}) collective-permute-start(bf16[1,3,16,192]{3,2,1,0:T(8,128)(2,1)S(1)} %slice_select_fusion.1), channel_id=1, source_target_pairs={{0,2},{2,0},{1,3},{3,1},{4,6},{6,4},{5,7},{7,5},{8,10},{10,8},{9,1... | collective-permute-start | bytes 55304 | tf_op jit(solution)/shard_map/ppermute | solution.py:33
  5.5 1.0 %fusion.68 = (f32[1,1,192]{2,1,0:T(1,128)S(1)}, f32[1,1,192]{2,1,0:T(1,128)S(1)}, f32[1,1,192]{2,1,0:T(1,128)S(1)}, f32[1,1,192]{2,1,0:T(1,128)S(1)}, f32[1,1,19...) fusion(f32[7,7,192]{2,1,0:T(8,128)} %param.15), kind=kLoop, calls=%fused_computation.228 | loop fusion | bytes 29184 | tf_op jit(solution)/shard_map/slice | solution.py:125
  6.6 1.0 %fusion.69 = (f32[1,1,192]{2,1,0:T(1,128)S(1)}, f32[1,1,192]{2,1,0:T(1,128)S(1)}, f32[1,1,192]{2,1,0:T(1,128)S(1)}, f32[1,1,192]{2,1,0:T(1,128)S(1)}, f32[1,1,19...) fusion(f32[7,7,192]{2,1,0:T(8,128)} %param.15), kind=kLoop, calls=%fused_computation.229 | loop fusion | bytes 29184 | tf_op jit(solution)/shard_map/slice | solution.py:125
  7.9 1.6 %collective-permute-start.1 = (bf16[1,22,3,192]{3,2,1,0:T(4,128)(2,1)S(1)}, bf16[1,22,3,192]{3,2,1,0:T(4,128)(2,1)S(1)}, u32[]{:S(2)}, u32[]{:S(2)}) collective-permute-start(bf16[1,22,3,192]{3,2,1,0:T(4,128)(2,1)S(1)} %get-tuple-element.93), channel_id=1, source_target_pairs={{0,4},{4,8},{8,12},{12,0},{1,5},{5,9},{9,13},{13,1},{2,6},{6,10},{... | collective-permute-start | bytes 76040 | tf_op jit(solution)/shard_map/ppermute | solution.py:21
  9.5 2.2 %collective-permute-start.2 = (bf16[1,22,3,192]{3,2,1,0:T(4,128)(2,1)S(1)}, bf16[1,22,3,192]{3,2,1,0:T(4,128)(2,1)S(1)}, u32[]{:S(2)}, u32[]{:S(2)}) collective-permute-start(bf16[1,22,3,192]{3,2,1,0:T(4,128)(2,1)S(1)} %get-tuple-element.94), channel_id=1, source_target_pairs={{4,0},{8,4},{12,8},{0,12},{5,1},{9,5},{13,9},{1,13},{6,2},{10,6},{... | collective-permute-start | bytes 76040 | tf_op jit(solution)/shard_map/ppermute | solution.py:24
  11.8 1.5 %fusion.70 = (f32[1,1,192]{2,1,0:T(1,128)S(1)}, f32[1,1,192]{2,1,0:T(1,128)S(1)}, f32[1,1,192]{2,1,0:T(1,128)S(1)}, f32[1,1,192]{2,1,0:T(1,128)S(1)}, f32[1,1,19...) fusion(f32[7,7,192]{2,1,0:T(8,128)} %param.15), kind=kLoop, calls=%fused_computation.230 | loop fusion | bytes 16896 | tf_op jit(solution)/shard_map/slice | solution.py:125
  13.3 0.8 %collective-permute-done.1 = bf16[1,22,3,192]{3,2,1,0:T(4,128)(2,1)S(1)} collective-permute-done((bf16[1,22,3,192]{3,2,1,0:T(4,128)(2,1)S(1)}, bf16[1,22,3,192]{3,2,1,0:T(4,128)(2,1)S(1)}, u32[]{:S(2)}, u32[]{:S(2)}) %collective-permute-start.1) | collective-permute-done | bytes 25376 | tf_op jit(solution)/shard_map/ppermute | solution.py:21
  14.4 2.5 %fusion.63 = (f32[16,16]{1,0:T(8,128)S(1)}, f32[1,16,16,192]{3,2,1,0:T(8,128)S(1)}) fusion(f32[192]{0:T(256)S(1)} %copy-done.89, f32[192]{0:T(256)S(1)} %bitcast.240, f32[1,22,22,192]{3,2,1,0:T(8,128)S(1)} %maximum_convert_fusion, f32[192]{0:T(256)} %bitcast.47, f32[192]{0:T(256)S(1)} %bitcast.148, f32[192]{0:T(256)S(1)} %bitcast.150, f32[192]{0:T(256)S(1)} %bitcast.152, ...), kind=kLoop, calls=%fused_computation.223 | loop fusion | flops 4865792 | bytes 9869824 | tf_op jit(solution)/shard_map/reduce_sum | solution.py:210
  17.3 0.2 multiply_reduce_fusion.52
  17.5 0.1 add_convert_fusion
  17.7 0.3 convolution_add_fusion
  18.0 0.4 convolution_add_fusion.1
  18.5 0.3 copy-done.3
  18.9 1.4 %multiply_reduce_fusion = (f32[192]{0:T(256)}, f32[1,16,16,192]{3,2,1,0:T(8,128)S(1)}, bf16[1,16,16,192]{3,2,1,0:T(8,128)(2,1)}) fusion(f32[192]{0:T(256)S(1)} %copy-done.91, f32[16,16]{1,0:T(8,128)S(1)} %get-tuple-element.151, bf16[1,16,16,192]{3,2,1,0:T(8,128)(2,1)S(1)} %copy-done.3, f32[256,192]{1,0:T(8,128)S(1)} %copy.27, ...), kind=kLoop, calls=%fused_computation.119 | loop fusion | flops 491328 | bytes 691200 | tf_op jit(solution)/shard_map/reduce_sum | solution.py:182
  20.3 1.3 %fusion.72 = (f32[768]{0:T(1024)}, bf16[256,768]{1,0:T(8,128)(2,1)S(1)}) fusion(f32[256,768]{1,0:T(8,128)S(1)} %convolution_add_fusion, bf16[768,192]{0,1:T(8,128)(2,1)S(1)} %copy-done, f32[256,192]{1,0:T(8,128)S(1)} %bitcast.143, f32[192]{0:T(256)S(1)} %copy-done.91), kind=kOutput, calls=%fused_computation.232 | convolution fusion | flops 79723776 | bytes 1675008 | tf_op jit(solution)/shard_map/dot_general | solution.py:174
  21.6 1.0 %fusion.62 = (f32[192]{0:T(256)}, f32[256]{0:T(256)S(1)}, f32[256,192]{0,1:T(8,128)S(1)}) fusion(f32[192]{0:T(256)S(1)} %copy-done.6, bf16[192,768]{1,0:T(8,128)(2,1)S(1)} %copy-done.1, bf16[256,768]{1,0:T(8,128)(2,1)S(1)} %get-tuple-element.155), kind=kOutput, calls=%fused_computation.222 | convolution fusion | flops 75644480 | bytes 887296 | tf_op jit(solution)/shard_map/dot_general | solution.py:177
  22.7 0.2 multiply_reduce_fusion.1
  23.0 0.7 multiply_reduce_fusion.2
  23.7 0.6 multiply_reduce_fusion.20
  24.2 1.0 %multiply_reduce_fusion.38 = (f32[192]{0:T(256)S(1)}, f32[192]{0:T(256)S(1)}, f32[192]{0:T(256)S(1)}, f32[192]{0:T(256)S(1)}, f32[192]{0:T(256)S(1)}, /*index=5*...) fusion(f32[1,16,16,192]{3,2,1,0:T(8,128)S(1)} %get-tuple-elemen, ...), kind=kLoop, calls=%fused_computation.157 | loop fusion | flops 1324416 | bytes 2763264 | tf_op jit(solution)/shard_map/reduce_sum | solution.py:150
  25.4 1.2 %fusion.61 = f32[192,768]{1,0:T(8,128)} fusion(f32[256,192]{1,0:T(8,128)S(1)} %bitcast.145, f32[192]{0:T(256)S(1)} %copy-done.92, f32[256,768]{1,0:T(8,128)S(1)} %convolution_add_fusion), kind=kOutput, calls=%fused_computation.190 | convolution fusion | flops 77365248 | bytes 1573632 | tf_op jit(solution)/shard_map/dot_general | solution.py:181
  26.6 0.3 fusion.57
  26.9 0.7 %stack.214 = f32[7,192]{1,0:T(8,128)S(1)} concatenate(f32[1,192]{1,0:T(1,128)} %bitcast.295, f32[1,192]{1,0:T(1,128)} %bitcast.294, f32[1,192]{1,0:T(1,128)} %bitcast.293, f32[1,192]{1,0:T(1,128)} %bitcast.292, f32[1,192]{1,0:T(1,128)} %bitcast.291, f32[1,192]{1,0:T(1,128)S(1)} %bitcast.290, f32[1,192]{1,0:T(1,128)S(1)} %bitcast.289), dimensions={0} | concatenate | bytes 10752 | tf_op jit(solution)/shard_map/stack | solution.py:148
  28.4 0.3 concatenate.45
  28.8 1.6 %collective-permute-done.6 = bf16[640,256]{1,0:T(8,128)(2,1)S(1)} collective-permute-done((bf16[640,256]{1,0:T(8,128)(2,1)S(1)}, bf16[640,256]{1,0:T(8,128)(2,1)S(1)}, u32[]{:S(2)}, u32[]{:S(2)}) %collective-permute-start.6) | collective-permute-done | bytes 327712 | tf_op jit(solution)/shard_map/ppermute | solution.py:78
  30.5 1.4 %collective-permute-start.7 = (bf16[320,256]{1,0:T(8,128)(2,1)S(1)}, bf16[320,256]{1,0:T(8,128)(2,1)S(1)}, u32[]{:S(2)}, u32[]{:S(2)}) collective-permute-start(bf16[320,256]{1,0:T(8,128)(2,1)S(1)} %dynamic-slice_convert_fusion.1), channel_id=1, source_target_pairs={{0,2},{2,0},{1,3},{3,1},{4,6},{6,4},{5,7},{7,5},{8,10},{10,8},{9,1... | collective-permute-start | bytes 491528 | tf_op jit(solution)/shard_map/ppermute | solution.py:78
  32.0 0.7 collective-permute-start.3
  32.6 4.5 %collective-permute-done.7 = bf16[320,256]{1,0:T(8,128)(2,1)S(1)} collective-permute-done((bf16[320,256]{1,0:T(8,128)(2,1)S(1)}, bf16[320,256]{1,0:T(8,128)(2,1)S(1)}, u32[]{:S(2)}, u32[]{:S(2)}) %collective-permute-start.7) | collective-permute-done | bytes 163872 | tf_op jit(solution)/shard_map/ppermute | solution.py:78
  37.2 3.5 %collective-permute-start.10 = (bf16[80,256]{1,0:T(8,128)(2,1)S(1)}, bf16[80,256]{1,0:T(8,128)(2,1)S(1)}, u32[]{:S(2)}, u32[]{:S(2)}) collective-permute-start(bf16[80,256]{1,0:T(8,128)(2,1)S(1)} %get-tuple-element.88), channel_id=1, source_target_pairs={{0,12},{4,8},{8,4},{12,0},{1,13},{5,9},{9,5},{13,1},{2,14},{6,10},... | collective-permute-start | bytes 122888 | tf_op jit(solution)/shard_map/ppermute | solution.py:78
  40.7 0.9 %collective-permute-start.9 = (bf16[80,256]{1,0:T(8,128)(2,1)S(1)}, bf16[80,256]{1,0:T(8,128)(2,1)S(1)}, u32[]{:S(2)}, u32[]{:S(2)}) collective-permute-start(bf16[80,256]{1,0:T(8,128)(2,1)S(1)} %get-tuple-element.89), channel_id=1, source_target_pairs={{0,8},{4,12},{8,0},{12,4},{1,9},{5,13},{9,1},{13,5},{2,10},{6,14},... | collective-permute-start | bytes 122888 | tf_op jit(solution)/shard_map/ppermute | solution.py:78
  41.6 1.4 %collective-permute-done.10 = bf16[80,256]{1,0:T(8,128)(2,1)S(1)} collective-permute-done((bf16[80,256]{1,0:T(8,128)(2,1)S(1)}, bf16[80,256]{1,0:T(8,128)(2,1)S(1)}, u32[]{:S(2)}, u32[]{:S(2)}) %collective-permute-start.10) | collective-permute-done | bytes 40992 | tf_op jit(solution)/shard_map/ppermute | solution.py:78
  43.0 1.6 %collective-permute-done.8 = bf16[80,256]{1,0:T(8,128)(2,1)S(1)} collective-permute-done((bf16[80,256]{1,0:T(8,128)(2,1)S(1)}, bf16[80,256]{1,0:T(8,128)(2,1)S(1)}, u32[]{:S(2)}, u32[]{:S(2)}) %collective-permute-start.8) | collective-permute-done | bytes 40992 | tf_op jit(solution)/shard_map/ppermute | solution.py:78
  44.7 0.9 %collective-permute-done.9 = bf16[80,256]{1,0:T(8,128)(2,1)S(1)} collective-permute-done((bf16[80,256]{1,0:T(8,128)(2,1)S(1)}, bf16[80,256]{1,0:T(8,128)(2,1)S(1)}, u32[]{:S(2)}, u32[]{:S(2)}) %collective-permute-start.9) | collective-permute-done | bytes 40992 | tf_op jit(solution)/shard_map/ppermute | solution.py:78
  46.0 2.2 %collective-permute-start.11 = (bf16[80,256]{1,0:T(8,128)(2,1)S(1)}, bf16[80,256]{1,0:T(8,128)(2,1)S(1)}, u32[]{:S(2)}, u32[]{:S(2)}) collective-permute-start(bf16[80,256]{1,0:T(8,128)(2,1)S(1)} %get-tuple-element.66), channel_id=1, source_target_pairs={{0,4},{4,0},{8,12},{12,8},{1,5},{5,1},{9,13},{13,9},{2,6},{6,2},{1... | collective-permute-start | bytes 122888 | tf_op jit(solution)/shard_map/ppermute | solution.py:92
  48.4 3.8 %collective-permute-start.5 = (bf16[1,22,3,192]{3,2,1,0:T(4,128)(2,1)S(1)}, bf16[1,22,3,192]{3,2,1,0:T(4,128)(2,1)S(1)}, u32[]{:S(2)}, u32[]{:S(2)}) collective-permute-start(bf16[1,22,3,192]{3,2,1,0:T(4,128)(2,1)S(1)} %get-tuple-element.92), channel_id=1, source_target_pairs={{4,0},{8,4},{12,8},{0,12},{5,1},{9,5},{13,9},{1,13},{6,2},{10,6},{... | collective-permute-start | bytes 76040 | tf_op jit(solution)/shard_map/ppermute | solution.py:24
  52.2 0.6 collective-permute-start.13
  52.8 4.3 %collective-permute-done.12 = bf16[80,256]{1,0:T(8,128)(2,1)S(1)} collective-permute-done((bf16[80,256]{1,0:T(8,128)(2,1)S(1)}, bf16[80,256]{1,0:T(8,128)(2,1)S(1)}, u32[]{:S(2)}, u32[]{:S(2)}) %collective-permute-start.12) | collective-permute-done | bytes 40992 | tf_op jit(solution)/shard_map/ppermute | solution.py:92
  57.1 0.9 %collective-permute-done.13 = bf16[80,256]{1,0:T(8,128)(2,1)S(1)} collective-permute-done((bf16[80,256]{1,0:T(8,128)(2,1)S(1)}, bf16[80,256]{1,0:T(8,128)(2,1)S(1)}, u32[]{:S(2)}, u32[]{:S(2)}) %collective-permute-start.13) | collective-permute-done | bytes 40992 | tf_op jit(solution)/shard_map/ppermute | solution.py:92
  58.0 1.5 %collective-permute-start.14 = (bf16[320,256]{1,0:T(8,128)(2,1)S(1)}, bf16[320,256]{1,0:T(8,128)(2,1)S(1)}, u32[]{:S(2)}, u32[]{:S(2)}) collective-permute-start(bf16[320,256]{1,0:T(8,128)(2,1)S(1)} %constant_dynamic-update-slice_fusion.11), channel_id=1, source_target_pairs={{0,2},{2,0},{1,3},{3,1},{4,6},{6,4},{5,7},{7,5},{8,10},{10,8},{9,1... | collective-permute-start | bytes 491528 | tf_op jit(solution)/shard_map/ppermute | solution.py:92
  59.7 3.7 %collective-permute-done.14 = bf16[320,256]{1,0:T(8,128)(2,1)S(1)} collective-permute-done((bf16[320,256]{1,0:T(8,128)(2,1)S(1)}, bf16[320,256]{1,0:T(8,128)(2,1)S(1)}, u32[]{:S(2)}, u32[]{:S(2)}) %collective-permute-start.14) | collective-permute-done | bytes 163872 | tf_op jit(solution)/shard_map/ppermute | solution.py:92
  63.8 3.3 %fusion.9 = bf16[1,16,16,192]{3,2,1,0:T(8,128)(2,1)} fusion(f32[1,22,22,192]{3,2,1,0:T(8,128)S(1)} %maximum_convert_fusion.1, f32[192]{0:T(256)S(1)} %bitcast.241, f32[192]{0:T(256)} %bitcast.47, f32[192]{0:T(256)S(1)} %bitcast.149, f32[192]{0:T(256)S(1)} %bitcast.151, f32[192]{0:T(256)S(1)} %bitcast.153, f32[192]{0:T(256)S(1)} %bitcast.155, ...), kind=kLoop, calls=%fused_computation.23 | loop fusion | flops 5013504 | bytes 9869056 | tf_op jit(solution)/shard_map/convert_element_type | solution.py:242
  67.4 0.6 fusion.64
  68.0 0.6 reshape.380
  68.6 0.7 reshape.381
  69.3 0.9 %maximum_bitcast_fusion = f32[768,192]{0,1:T(8,128)} fusion(f32[192,256]{1,0:T(8,128)S(1)} %get-tuple-element.77, f32[192,256]{1,0:T(8,128)S(1)} %get-tuple-element.76, f32[192,256]{1,0:T(8,128)S(1)} %get-tuple-element.75), kind=kLoop, calls=%fused_computation.14 | loop fusion | flops 294912 | bytes 1179648 | tf_op jit(solution)/shard_map/transpose | solution.py:271
  70.1 0.9 %pad_maximum_fusion = f32[192,768]{1,0:T(8,128)} fusion(f32[192,256]{1,0:T(8,128)S(1)} %get-tuple-element.80, f32[192,256]{1,0:T(8,128)S(1)} %get-tuple-element.79, f32[192,256]{1,0:T(8,128)S(1)} %get-tuple-element.78), kind=kLoop, calls=%fused_computation.13 | loop fusion | flops 294912 | bytes 1179648 | tf_op jit(solution)/shard_map/concatenate | solution.py:54
  (254 shorter events, 2.7 us)
Async XLA Ops:
  2.5 5.4 %collective-permute-start = (bf16[1,3,16,192]{3,2,1,0:T(8,128)(2,1)S(1)}, bf16[1,3,16,192]{3,2,1,0:T(8,128)(2,1)S(1)}, u32[]{:S(2)}, u32[]{:S(2)}) collective-permute-start(bf16[1,3,16,192]{3,2,1,0:T(8,128)(2,1)S(1)} %slice_select_fusion.1), channel_id=1, source_target_pairs={{0,2},{2,0},{1,3},{3,1},{4,6},{6,4},{5,7},{7,5},{8,10},{10,8},{9,1... | collective-permute-start | bytes 55304 | tf_op jit(solution)/shard_map/ppermute | solution.py:33
  7.9 6.3 %collective-permute-start.1 = (bf16[1,22,3,192]{3,2,1,0:T(4,128)(2,1)S(1)}, bf16[1,22,3,192]{3,2,1,0:T(4,128)(2,1)S(1)}, u32[]{:S(2)}, u32[]{:S(2)}) collective-permute-start(bf16[1,22,3,192]{3,2,1,0:T(4,128)(2,1)S(1)} %get-tuple-element.93), channel_id=1, source_target_pairs={{0,4},{4,8},{8,12},{12,0},{1,5},{5,9},{9,13},{13,1},{2,6},{6,10},{... | collective-permute-start | bytes 76040 | tf_op jit(solution)/shard_map/ppermute | solution.py:21
  9.5 4.6 %collective-permute-start.2 = (bf16[1,22,3,192]{3,2,1,0:T(4,128)(2,1)S(1)}, bf16[1,22,3,192]{3,2,1,0:T(4,128)(2,1)S(1)}, u32[]{:S(2)}, u32[]{:S(2)}) collective-permute-start(bf16[1,22,3,192]{3,2,1,0:T(4,128)(2,1)S(1)} %get-tuple-element.94), channel_id=1, source_target_pairs={{4,0},{8,4},{12,8},{0,12},{5,1},{9,5},{13,9},{1,13},{6,2},{10,6},{... | collective-permute-start | bytes 76040 | tf_op jit(solution)/shard_map/ppermute | solution.py:24
  28.7 1.7 %collective-permute-start.6 = (bf16[640,256]{1,0:T(8,128)(2,1)S(1)}, bf16[640,256]{1,0:T(8,128)(2,1)S(1)}, u32[]{:S(2)}, u32[]{:S(2)}) collective-permute-start(bf16[640,256]{1,0:T(8,128)(2,1)S(1)} %dynamic-slice_convert_fusion), channel_id=1, source_target_pairs={{0,1},{1,0},{2,3},{3,2},{4,5},{5,4},{6,7},{7,6},{8,9},{9,8},{10,11... | collective-permute-start | bytes 983048 | tf_op jit(solution)/shard_map/ppermute | solution.py:78
  30.5 6.6 %collective-permute-start.7 = (bf16[320,256]{1,0:T(8,128)(2,1)S(1)}, bf16[320,256]{1,0:T(8,128)(2,1)S(1)}, u32[]{:S(2)}, u32[]{:S(2)}) collective-permute-start(bf16[320,256]{1,0:T(8,128)(2,1)S(1)} %dynamic-slice_convert_fusion.1), channel_id=1, source_target_pairs={{0,2},{2,0},{1,3},{3,1},{4,6},{6,4},{5,7},{7,5},{8,10},{10,8},{9,1... | collective-permute-start | bytes 491528 | tf_op jit(solution)/shard_map/ppermute | solution.py:78
  32.0 9.7 %collective-permute-start.3 = (bf16[1,3,16,192]{3,2,1,0:T(8,128)(2,1)S(1)}, bf16[1,3,16,192]{3,2,1,0:T(8,128)(2,1)S(1)}, u32[]{:S(2)}, u32[]{:S(2)}) collective-permute-start(bf16[1,3,16,192]{3,2,1,0:T(8,128)(2,1)S(1)} %slice_select_fusion), channel_id=1, source_target_pairs={{0,2},{2,0},{1,3},{3,1},{4,6},{6,4},{5,7},{7,5},{8,10},{10,8},{9,1... | collective-permute-start | bytes 55304 | tf_op jit(solution)/shard_map/ppermute | solution.py:33
  37.2 5.9 %collective-permute-start.10 = (bf16[80,256]{1,0:T(8,128)(2,1)S(1)}, bf16[80,256]{1,0:T(8,128)(2,1)S(1)}, u32[]{:S(2)}, u32[]{:S(2)}) collective-permute-start(bf16[80,256]{1,0:T(8,128)(2,1)S(1)} %get-tuple-element.88), channel_id=1, source_target_pairs={{0,12},{4,8},{8,4},{12,0},{1,13},{5,9},{9,5},{13,1},{2,14},{6,10},... | collective-permute-start | bytes 122888 | tf_op jit(solution)/shard_map/ppermute | solution.py:78
  40.7 4.0 %collective-permute-start.8 = (bf16[80,256]{1,0:T(8,128)(2,1)S(1)}, bf16[80,256]{1,0:T(8,128)(2,1)S(1)}, u32[]{:S(2)}, u32[]{:S(2)}) collective-permute-start(bf16[80,256]{1,0:T(8,128)(2,1)S(1)} %get-tuple-element.87), channel_id=1, source_target_pairs={{0,4},{4,0},{8,12},{12,8},{1,5},{5,1},{9,13},{13,9},{2,6},{6,2},{1... | collective-permute-start | bytes 122888 | tf_op jit(solution)/shard_map/ppermute | solution.py:78
  40.7 4.9 %collective-permute-start.9 = (bf16[80,256]{1,0:T(8,128)(2,1)S(1)}, bf16[80,256]{1,0:T(8,128)(2,1)S(1)}, u32[]{:S(2)}, u32[]{:S(2)}) collective-permute-start(bf16[80,256]{1,0:T(8,128)(2,1)S(1)} %get-tuple-element.89), channel_id=1, source_target_pairs={{0,8},{4,12},{8,0},{12,4},{1,9},{5,13},{9,1},{13,5},{2,10},{6,14},... | collective-permute-start | bytes 122888 | tf_op jit(solution)/shard_map/ppermute | solution.py:78
  45.6 17.8 %copy-start.4 = (bf16[1,16,16,192]{3,2,1,0:T(8,128)(2,1)S(1)}, bf16[1,16,16,192]{3,2,1,0:T(8,128)(2,1)}, u32[]{:S(2)}) copy-start(bf16[1,16,16,192]{3,2,1,0:T(8,128)(2,1)} %param.13) | copy-start | bytes 294916
  45.6 17.8 %copy-start.8 = (f32[1,1,192]{2,1,0:T(1,128)S(1)}, f32[1,1,192]{2,1,0:T(1,128)}, u32[]{:S(2)}) copy-start(f32[1,1,192]{2,1,0:T(1,128)} %copy-done.7) | copy-start | bytes 2308
  45.6 17.8 %copy-start.10 = (f32[1,1,192]{2,1,0:T(1,128)S(1)}, f32[1,1,192]{2,1,0:T(1,128)}, u32[]{:S(2)}) copy-start(f32[1,1,192]{2,1,0:T(1,128)} %copy-done.9) | copy-start | bytes 2308
  45.6 17.8 %copy-start.12 = (f32[1,1,192]{2,1,0:T(1,128)S(1)}, f32[1,1,192]{2,1,0:T(1,128)}, u32[]{:S(2)}) copy-start(f32[1,1,192]{2,1,0:T(1,128)} %copy-done.11) | copy-start | bytes 2308
  45.6 17.8 %copy-start.14 = (f32[1,1,192]{2,1,0:T(1,128)S(1)}, f32[1,1,192]{2,1,0:T(1,128)}, u32[]{:S(2)}) copy-start(f32[1,1,192]{2,1,0:T(1,128)} %copy-done.13) | copy-start | bytes 2308
  45.7 17.8 %copy-start.16 = (f32[1,1,192]{2,1,0:T(1,128)S(1)}, f32[1,1,192]{2,1,0:T(1,128)}, u32[]{:S(2)}) copy-start(f32[1,1,192]{2,1,0:T(1,128)} %copy-done.15) | copy-start | bytes 2308
  45.7 17.8 %copy-start.18 = (f32[1,1,192]{2,1,0:T(1,128)S(1)}, f32[1,1,192]{2,1,0:T(1,128)}, u32[]{:S(2)}) copy-start(f32[1,1,192]{2,1,0:T(1,128)} %copy-done.17) | copy-start | bytes 2308
  45.7 17.8 %copy-start.20 = (f32[1,1,192]{2,1,0:T(1,128)S(1)}, f32[1,1,192]{2,1,0:T(1,128)}, u32[]{:S(2)}) copy-start(f32[1,1,192]{2,1,0:T(1,128)} %copy-done.19) | copy-start | bytes 2308
  45.7 17.8 %copy-start.22 = (f32[1,1,192]{2,1,0:T(1,128)S(1)}, f32[1,1,192]{2,1,0:T(1,128)}, u32[]{:S(2)}) copy-start(f32[1,1,192]{2,1,0:T(1,128)} %copy-done.21) | copy-start | bytes 2308
  45.7 17.8 %copy-start.24 = (f32[1,1,192]{2,1,0:T(1,128)S(1)}, f32[1,1,192]{2,1,0:T(1,128)}, u32[]{:S(2)}) copy-start(f32[1,1,192]{2,1,0:T(1,128)} %copy-done.23) | copy-start | bytes 2308
  45.7 17.8 %copy-start.26 = (f32[1,1,192]{2,1,0:T(1,128)S(1)}, f32[1,1,192]{2,1,0:T(1,128)}, u32[]{:S(2)}) copy-start(f32[1,1,192]{2,1,0:T(1,128)} %copy-done.25) | copy-start | bytes 2308
  45.7 17.8 %copy-start.28 = (f32[1,1,192]{2,1,0:T(1,128)S(1)}, f32[1,1,192]{2,1,0:T(1,128)}, u32[]{:S(2)}) copy-start(f32[1,1,192]{2,1,0:T(1,128)} %copy-done.27) | copy-start | bytes 2308
  45.7 17.8 %copy-start.30 = (f32[1,1,192]{2,1,0:T(1,128)S(1)}, f32[1,1,192]{2,1,0:T(1,128)}, u32[]{:S(2)}) copy-start(f32[1,1,192]{2,1,0:T(1,128)} %copy-done.29) | copy-start | bytes 2308
  45.7 17.8 %copy-start.32 = (f32[1,1,192]{2,1,0:T(1,128)S(1)}, f32[1,1,192]{2,1,0:T(1,128)}, u32[]{:S(2)}) copy-start(f32[1,1,192]{2,1,0:T(1,128)} %copy-done.31) | copy-start | bytes 2308
  45.7 17.8 %copy-start.34 = (f32[1,1,192]{2,1,0:T(1,128)S(1)}, f32[1,1,192]{2,1,0:T(1,128)}, u32[]{:S(2)}) copy-start(f32[1,1,192]{2,1,0:T(1,128)} %copy-done.33) | copy-start | bytes 2308
  45.8 17.8 %copy-start.36 = (f32[1,1,192]{2,1,0:T(1,128)S(1)}, f32[1,1,192]{2,1,0:T(1,128)}, u32[]{:S(2)}) copy-start(f32[1,1,192]{2,1,0:T(1,128)} %copy-done.35) | copy-start | bytes 2308
  45.8 17.8 %copy-start.38 = (f32[1,1,192]{2,1,0:T(1,128)S(1)}, f32[1,1,192]{2,1,0:T(1,128)}, u32[]{:S(2)}) copy-start(f32[1,1,192]{2,1,0:T(1,128)} %copy-done.37) | copy-start | bytes 2308
  45.8 17.8 %copy-start.40 = (f32[1,1,192]{2,1,0:T(1,128)S(1)}, f32[1,1,192]{2,1,0:T(1,128)}, u32[]{:S(2)}) copy-start(f32[1,1,192]{2,1,0:T(1,128)} %copy-done.39) | copy-start | bytes 2308
  45.8 17.8 %copy-start.42 = (f32[1,1,192]{2,1,0:T(1,128)S(1)}, f32[1,1,192]{2,1,0:T(1,128)}, u32[]{:S(2)}) copy-start(f32[1,1,192]{2,1,0:T(1,128)} %copy-done.41) | copy-start | bytes 2308
  45.8 17.8 %copy-start.44 = (f32[1,1,192]{2,1,0:T(1,128)S(1)}, f32[1,1,192]{2,1,0:T(1,128)}, u32[]{:S(2)}) copy-start(f32[1,1,192]{2,1,0:T(1,128)} %copy-done.43) | copy-start | bytes 2308
  45.8 17.8 %copy-start.46 = (f32[1,1,192]{2,1,0:T(1,128)S(1)}, f32[1,1,192]{2,1,0:T(1,128)}, u32[]{:S(2)}) copy-start(f32[1,1,192]{2,1,0:T(1,128)} %copy-done.45) | copy-start | bytes 2308
  45.8 17.8 %copy-start.48 = (f32[1,1,192]{2,1,0:T(1,128)S(1)}, f32[1,1,192]{2,1,0:T(1,128)}, u32[]{:S(2)}) copy-start(f32[1,1,192]{2,1,0:T(1,128)} %copy-done.47) | copy-start | bytes 2308
  45.8 17.8 %copy-start.50 = (f32[1,1,192]{2,1,0:T(1,128)S(1)}, f32[1,1,192]{2,1,0:T(1,128)}, u32[]{:S(2)}) copy-start(f32[1,1,192]{2,1,0:T(1,128)} %copy-done.49) | copy-start | bytes 2308
  45.8 17.8 %copy-start.52 = (f32[1,1,192]{2,1,0:T(1,128)S(1)}, f32[1,1,192]{2,1,0:T(1,128)}, u32[]{:S(2)}) copy-start(f32[1,1,192]{2,1,0:T(1,128)} %copy-done.51) | copy-start | bytes 2308
  45.8 17.8 %copy-start.54 = (f32[1,1,192]{2,1,0:T(1,128)S(1)}, f32[1,1,192]{2,1,0:T(1,128)}, u32[]{:S(2)}) copy-start(f32[1,1,192]{2,1,0:T(1,128)} %copy-done.53) | copy-start | bytes 2308
  45.9 17.8 %copy-start.56 = (f32[1,1,192]{2,1,0:T(1,128)S(1)}, f32[1,1,192]{2,1,0:T(1,128)}, u32[]{:S(2)}) copy-start(f32[1,1,192]{2,1,0:T(1,128)} %copy-done.55) | copy-start | bytes 2308
  45.9 17.8 %copy-start.58 = (f32[1,1,192]{2,1,0:T(1,128)S(1)}, f32[1,1,192]{2,1,0:T(1,128)}, u32[]{:S(2)}) copy-start(f32[1,1,192]{2,1,0:T(1,128)} %copy-done.57) | copy-start | bytes 2308
  45.9 17.8 %copy-start.60 = (f32[1,1,192]{2,1,0:T(1,128)S(1)}, f32[1,1,192]{2,1,0:T(1,128)}, u32[]{:S(2)}) copy-start(f32[1,1,192]{2,1,0:T(1,128)} %copy-done.59) | copy-start | bytes 2308
  45.9 17.8 %copy-start.62 = (f32[1,1,192]{2,1,0:T(1,128)S(1)}, f32[1,1,192]{2,1,0:T(1,128)}, u32[]{:S(2)}) copy-start(f32[1,1,192]{2,1,0:T(1,128)} %copy-done.61) | copy-start | bytes 2308
  45.9 17.8 %copy-start.64 = (f32[1,1,192]{2,1,0:T(1,128)S(1)}, f32[1,1,192]{2,1,0:T(1,128)}, u32[]{:S(2)}) copy-start(f32[1,1,192]{2,1,0:T(1,128)} %copy-done.63) | copy-start | bytes 2308
  45.9 17.8 %copy-start.66 = (f32[1,1,192]{2,1,0:T(1,128)S(1)}, f32[1,1,192]{2,1,0:T(1,128)}, u32[]{:S(2)}) copy-start(f32[1,1,192]{2,1,0:T(1,128)} %copy-done.65) | copy-start | bytes 2308
  45.9 17.8 %copy-start.68 = (f32[1,1,192]{2,1,0:T(1,128)S(1)}, f32[1,1,192]{2,1,0:T(1,128)}, u32[]{:S(2)}) copy-start(f32[1,1,192]{2,1,0:T(1,128)} %copy-done.67) | copy-start | bytes 2308
  46.0 6.8 %collective-permute-start.11 = (bf16[80,256]{1,0:T(8,128)(2,1)S(1)}, bf16[80,256]{1,0:T(8,128)(2,1)S(1)}, u32[]{:S(2)}, u32[]{:S(2)}) collective-permute-start(bf16[80,256]{1,0:T(8,128)(2,1)S(1)} %get-tuple-element.66), channel_id=1, source_target_pairs={{0,4},{4,0},{8,12},{12,8},{1,5},{5,1},{9,13},{13,9},{2,6},{6,2},{1... | collective-permute-start | bytes 122888 | tf_op jit(solution)/shard_map/ppermute | solution.py:92
  48.3 11.2 %collective-permute-start.4 = (bf16[1,22,3,192]{3,2,1,0:T(4,128)(2,1)S(1)}, bf16[1,22,3,192]{3,2,1,0:T(4,128)(2,1)S(1)}, u32[]{:S(2)}, u32[]{:S(2)}) collective-permute-start(bf16[1,22,3,192]{3,2,1,0:T(4,128)(2,1)S(1)} %get-tuple-element.91), channel_id=1, source_target_pairs={{0,4},{4,8},{8,12},{12,0},{1,5},{5,9},{9,13},{13,1},{2,6},{6,10},{... | collective-permute-start | bytes 76040 | tf_op jit(solution)/shard_map/ppermute | solution.py:21
  48.4 11.1 %collective-permute-start.5 = (bf16[1,22,3,192]{3,2,1,0:T(4,128)(2,1)S(1)}, bf16[1,22,3,192]{3,2,1,0:T(4,128)(2,1)S(1)}, u32[]{:S(2)}, u32[]{:S(2)}) collective-permute-start(bf16[1,22,3,192]{3,2,1,0:T(4,128)(2,1)S(1)} %get-tuple-element.92), channel_id=1, source_target_pairs={{4,0},{8,4},{12,8},{0,12},{5,1},{9,5},{13,9},{1,13},{6,2},{10,6},{... | collective-permute-start | bytes 76040 | tf_op jit(solution)/shard_map/ppermute | solution.py:24
  52.2 4.9 %collective-permute-start.12 = (bf16[80,256]{1,0:T(8,128)(2,1)S(1)}, bf16[80,256]{1,0:T(8,128)(2,1)S(1)}, u32[]{:S(2)}, u32[]{:S(2)}) collective-permute-start(bf16[80,256]{1,0:T(8,128)(2,1)S(1)} %get-tuple-element.66), channel_id=1, source_target_pairs={{0,8},{4,12},{8,0},{12,4},{1,9},{5,13},{9,1},{13,5},{2,10},{6,14},... | collective-permute-start | bytes 122888 | tf_op jit(solution)/shard_map/ppermute | solution.py:92
  52.2 5.8 %collective-permute-start.13 = (bf16[80,256]{1,0:T(8,128)(2,1)S(1)}, bf16[80,256]{1,0:T(8,128)(2,1)S(1)}, u32[]{:S(2)}, u32[]{:S(2)}) collective-permute-start(bf16[80,256]{1,0:T(8,128)(2,1)S(1)} %get-tuple-element.66), channel_id=1, source_target_pairs={{0,12},{4,8},{8,4},{12,0},{1,13},{5,9},{9,5},{13,1},{2,14},{6,10},... | collective-permute-start | bytes 122888 | tf_op jit(solution)/shard_map/ppermute | solution.py:92
  58.0 5.3 %collective-permute-start.14 = (bf16[320,256]{1,0:T(8,128)(2,1)S(1)}, bf16[320,256]{1,0:T(8,128)(2,1)S(1)}, u32[]{:S(2)}, u32[]{:S(2)}) collective-permute-start(bf16[320,256]{1,0:T(8,128)(2,1)S(1)} %constant_dynamic-update-slice_fusion.11), channel_id=1, source_target_pairs={{0,2},{2,0},{1,3},{3,1},{4,6},{6,4},{5,7},{7,5},{8,10},{10,8},{9,1... | collective-permute-start | bytes 491528 | tf_op jit(solution)/shard_map/ppermute | solution.py:92
  63.4 3.9 %collective-permute-start.15 = (bf16[640,256]{1,0:T(8,128)(2,1)S(1)}, bf16[640,256]{1,0:T(8,128)(2,1)S(1)}, u32[]{:S(2)}, u32[]{:S(2)}) collective-permute-start(bf16[640,256]{1,0:T(8,128)(2,1)S(1)} %constant_dynamic-update-slice_fusion.9), channel_id=1, source_target_pairs={{0,1},{1,0},{2,3},{3,2},{4,5},{5,4},{6,7},{7,6},{8,9},{9,8},{10,11... | collective-permute-start | bytes 983048 | tf_op jit(solution)/shard_map/ppermute | solution.py:92
  (62 other events, 516.7 us)

commit v2 on v1

--- a/solution.py
+++ b/solution.py
@@ -1,8 +1,11 @@
+import functools
 import math
 
 import jax
 import jax.numpy as jnp
 from jax import lax
+from jax.experimental import pallas as pl
+from jax.experimental.pallas import tpu as pltpu
 from jax.sharding import PartitionSpec as P
 
 EPS = 1e-06
@@ -287,9 +290,640 @@
     )
 
 
+VMEM = pl.BlockSpec(memory_space=pltpu.VMEM)
+HBM = pl.BlockSpec(memory_space=pltpu.HBM)
+PARAMS = pltpu.CompilerParams(vmem_limit_bytes=20 << 20)
+F32 = jnp.float32
+SLOT = 256
+STRIDE = 32
+CENTER = 8
+PAD_ROWS = 24
+ROOT_2_PI = math.sqrt(2 / math.pi)
+
+
+def call(kernel, outs, args, flops=0, scratch=(), hbm=(), hbm_out=()):
+    moved = sum(a.size * a.dtype.itemsize for a in args) + sum(
+        math.prod(s) * jnp.dtype(d).itemsize for s, d in outs
+    )
+    return pl.pallas_call(
+        kernel,
+        out_shape=tuple(jax.ShapeDtypeStruct(s, d) for s, d in outs),
+        in_specs=[HBM if i in hbm else VMEM for i in range(len(args))],
+        out_specs=tuple(HBM if i in hbm_out else VMEM for i in range(len(outs))),
+        scratch_shapes=list(scratch),
+        compiler_params=PARAMS,
+        cost_estimate=pl.CostEstimate(flops=flops, bytes_accessed=moved, transcendentals=0),
+    )(*args)
+
+
+def copies(pairs, sems):
+    started = [
+        pltpu.make_async_copy(source, target, sems.at[i]) for i, (source, target) in enumerate(pairs)
+    ]
+    for copy in started:
+        copy.start()
+    return started
+
+
+def dot(a, b, dims):
+    return lax.dot_general(a, b, (dims, ((), ())), preferred_element_type=F32)
+
+
+def tap_slots(taps):
+    return [((i // 24) * 8 + i % 8, ((i % 24) // 8) * SLOT) for i in range(taps)]
+
+
+def mask_full(mask_ref, cells, channels):
+    tile_w = mask_ref.shape[1]
+    index = lax.broadcasted_iota(jnp.int32, (cells, mask_ref.shape[0]), 0)
+    of_row = lax.div(index, tile_w) == lax.broadcasted_iota(jnp.int32, index.shape, 1)
+    mask = mask_ref[...].astype(F32).astype(LINK)
+    rows = dot(of_row.astype(F32).astype(LINK), mask, ((1,), (0,)))
+    index = lax.broadcasted_iota(jnp.int32, rows.shape, 0)
+    of_col = lax.rem(index, tile_w) == lax.broadcasted_iota(jnp.int32, rows.shape, 1)
+    picked = jnp.where(of_col, rows, 0.0).astype(LINK)
+    return dot(picked, jnp.ones((tile_w, channels), LINK), ((1,), (0,)))
+
+
+def prepare_kernel(tw, fields_hbm, mask_hbm, start_ref, edge_ref, full_ref, fields_ref, mask_ref, sems):
+    fetch = copies(((mask_hbm, mask_ref), (fields_hbm, fields_ref)), sems)
+    cells, channels = fields_ref.shape
+    fetch[0].wait()
+    full = mask_full(mask_ref, cells, channels)
+    full_ref[...] = full
+    fetch[1].wait()
+    start_ref[...] = (fields_ref[...].astype(F32) * full).astype(LINK)
+    first = lax.axis_index("lat") == 0
+    edge_ref[...] = jnp.where(first, start_ref[cells - 3 * tw :], start_ref[: 3 * tw])
+
+
+def load_kernel(full_ref, *refs):
+    count = (len(refs) - 3) // 2
+    sources, targets = refs[:count], refs[count : 2 * count]
+    branch_grad_ref, hidden_grad_ref, sems = refs[2 * count :]
+    fetch = copies(tuple(zip(sources, targets)), sems)
+    cot_ref, scale_ref, w_out_ref = targets[:3]
+    for copy in fetch[:3]:
+        copy.wait()
+    grad = (cot_ref[...].astype(F32) * full_ref[...] * scale_ref[...]).astype(LINK)
+    branch_grad_ref[...] = grad
+    hidden_grad_ref[...] = dot(grad, w_out_ref[...], ((1,), (0,)))
+    for copy in fetch[3:]:
+        copy.wait()
+
+
+def lane_tiles(channels):
+    return [(t, t * 128, min(128, channels - t * 128)) for t in range(-(-channels // 128))]
+
+
+def put_rows(padded_ref, row, values):
+    for t, lane, width in lane_tiles(values.shape[1]):
+        padded_ref[t, pl.ds(row, values.shape[0]), pl.ds(0, width)] = values[:, lane : lane + width]
+
+
+def fill_center(padded_ref, value_of_row, tile_h, tw, top, bottom):
+    for h in range(tile_h):
+        put_rows(padded_ref, (h + 3) * STRIDE + CENTER, value_of_row(h))
+    for r in range(3):
+        put_rows(padded_ref, r * STRIDE + CENTER, top(r))
+        put_rows(padded_ref, (tile_h + 3 + r) * STRIDE + CENTER, bottom(r))
+
+
+def write_edges(padded_ref, tw, channels, near_ref, far_ref, row):
+    even = lax.rem(lax.axis_index("lon"), 2) == 0
+    for c in range(3):
+        for t, lane, width in lane_tiles(channels):
+            left = padded_ref[t, pl.ds(CENTER + c, PAD_ROWS, stride=STRIDE), :]
+            right = padded_ref[t, pl.ds(CENTER + tw - 3 + c, PAD_ROWS, stride=STRIDE), :]
+            place = pl.ds(row, PAD_ROWS), pl.ds(c * SLOT + lane, width)
+            near_ref[place] = jnp.where(even, right, left)[:, :width].astype(LINK)
+            far_ref[place] = jnp.where(even, left, right)[:, :width].astype(LINK)
+
+
+def read_edges(padded_ref, tw, channels, near_ref, far_ref, row):
+    even = lax.rem(lax.axis_index("lon"), 2) == 0
+    for c in range(3):
+        for t, lane, width in lane_tiles(channels):
+            place = pl.ds(row, PAD_ROWS), pl.ds(c * SLOT + lane, 128)
+            near = near_ref[place].astype(F32)
+            far = far_ref[place].astype(F32)
+            left = pl.ds(CENTER - 3 + c, PAD_ROWS, stride=STRIDE)
+            right = pl.ds(CENTER + tw + c, PAD_ROWS, stride=STRIDE)
+            padded_ref[t, left, :] = jnp.where(even, far, near)
+            padded_ref[t, right, :] = jnp.where(even, near, far)
+
+
+def lat_rows(read, tw):
+    first = lax.axis_index("lat") == 0
+
+    def top(r):
+        rows = read(r).astype(F32)
+        return jnp.where(first, jnp.zeros_like(rows), rows)
+
+    def bottom(r):
+        rows = read(r).astype(F32)
+        return jnp.where(first, rows, jnp.zeros_like(rows))
+
+    return top, bottom
+
+
+def shift_all(padded_ref, shifts_ref, tile_h, tw):
+    for q in range(7):
+        for h in range(tile_h + 6):
+            for t, lane, width in lane_tiles(shifts_ref.shape[2]):
+                shifts_ref[q, pl.ds(h * tw, tw), pl.ds(lane, width)] = padded_ref[
+                    t, pl.ds(h * STRIDE + CENTER - 3 + q, tw), pl.ds(0, width)
+                ]
+
+
+def convolve(shifts_ref, kernel_ref, out_ref, tile_h, tw, flip):
+    block = 2
+
+    def step(i, carry):
+        base = pl.multiple_of(i * block * tw, 8)
+        total = jnp.zeros((block * tw, out_ref.shape[1]), F32)
+        for q in range(7):
+            rows = shifts_ref[q, pl.ds(base, (block + 6) * tw), :]
+            for r in range(7):
+                tap = kernel_ref[6 - r, 6 - q : 7 - q, :] if flip else kernel_ref[r, q : q + 1, :]
+                total = total + rows[r * tw : (r + block) * tw] * tap
+        out_ref[pl.ds(base, block * tw), :] = total
+        return carry
+
+    lax.fori_loop(0, tile_h // block, step, 0)
+
+
+def edges_kernel(tile_h, tw, start_ref, lat_ref, loaded_ref, near_ref, far_ref, padded_ref):
+    top, bottom = lat_rows(lambda r: lat_ref[pl.ds(r * tw, tw), :], tw)
+    fill_center(
+        padded_ref, lambda h: start_ref[pl.ds(h * tw, tw), :].astype(F32), tile_h, tw, top, bottom
+    )
+    write_edges(padded_ref, tw, start_ref.shape[1], near_ref, far_ref, 0)
+
+
+def inner_conv_kernel(
+    tile_h, tw, start_ref, lat_ref, kernel_ref, bias_ref, out_ref, padded_ref, shifts_ref, conv_ref
+):
+    top, bottom = lat_rows(lambda r: lat_ref[pl.ds(r * tw, tw), :], tw)
+    fill_center(
+        padded_ref, lambda h: start_ref[pl.ds(h * tw, tw), :].astype(F32), tile_h, tw, top, bottom
+    )
+    blank = jnp.zeros((PAD_ROWS, 128), F32)
+    for t in range(padded_ref.shape[0]):
+        for c in range(3):
+            padded_ref[t, pl.ds(CENTER - 3 + c, PAD_ROWS, stride=STRIDE), :] = blank
+            padded_ref[t, pl.ds(CENTER + tw + c, PAD_ROWS, stride=STRIDE), :] = blank
+    shift_all(padded_ref, shifts_ref, tile_h, tw)
+    convolve(shifts_ref, kernel_ref, conv_ref, tile_h, tw, False)
+    conv = conv_ref[...] + bias_ref[...]
+    for t, lane, width in lane_tiles(conv.shape[1]):
+        out_ref[t, :, pl.ds(0, width)] = conv[:, lane : lane + width]
+
+
+def add_columns(conv_ref, kernel_ref, near_ref, far_ref, tile_h, tw, channels):
+    even = lax.rem(lax.axis_index("lon"), 2) == 0
+    for t, lane, width in lane_tiles(channels):
+        left, right = [], []
+        for c in range(3):
+            place = pl.ds(0, PAD_ROWS), pl.ds(c * SLOT + lane, width)
+            near = near_ref[place].astype(F32)
+            far = far_ref[place].astype(F32)
+            left.append(jnp.where(even, far, near))
+            right.append(jnp.where(even, near, far))
+        for w in range(3):
+            for col, halo, taps in (
+                (w, left, [(q, w + q) for q in range(3 - w)]),
+                (tw - 1 - w, right, [(6 - q, 2 - w - q) for q in range(3 - w)]),
+            ):
+                rows = pl.ds(col, tile_h, stride=tw)
+                total = conv_ref[t, rows, :][:, :width]
+                for q, c in taps:
+                    for r in range(7):
+                        tap = kernel_ref[r, q : q + 1, pl.ds(lane, width)]
+                        total = total + halo[c][r : r + tile_h] * tap
+                conv_ref[t, rows, pl.ds(0, width)] = total
+
+
+def main_kernel(
+    tile_h, tw,
+    inner_ref, near_ref, far_ref, kernel_ref, gain_ref, ln_bias_ref, branch_grad_ref, hidden_grad_ref,
+    w_in_ref, b_in_ref,
+    send_ref, keep_ref, normed_ref, inv_std_ref, hidden_ref, pre_grad_ref, b_in_grad_ref,
+    conv_ref, grad_in_ref, grad_out_ref,
+):
+    channels, hid = w_in_ref.shape
+    conv_ref[...] = inner_ref[...]
+    add_columns(conv_ref, kernel_ref, near_ref, far_ref, tile_h, tw, channels)
+    conv = jnp.concatenate([conv_ref[t, :, :][:, :width] for t, _, width in lane_tiles(channels)], axis=1)
+    shifted = conv - jnp.mean(conv, axis=1, keepdims=True)
+    inv_std = lax.rsqrt(jnp.mean(shifted * shifted, axis=1, keepdims=True) + EPS)
+    normed = shifted * inv_std
+    normed_ref[...] = normed
+    inv_std_ref[...] = jnp.broadcast_to(inv_std, inv_std_ref.shape)
+    act = (normed * gain_ref[...] + ln_bias_ref[...]).astype(LINK)
+    branch_grad = branch_grad_ref[...]
+    width = 256
+    for j in range(hid // width):
+        cols = pl.ds(j * width, width)
+        pre = dot(act, w_in_ref[:, cols], ((1,), (0,))) + b_in_ref[cols][None, :]
+        square = pre * pre
+        tanh = jnp.tanh(ROOT_2_PI * (pre + 0.044715 * (pre * square)))
+        half = 0.5 * (1.0 + tanh)
+        hidden = (pre * half).astype(LINK)
+        slope = half + (0.5 * ROOT_2_PI) * pre * (1.0 - tanh * tanh) * (1.0 + (3 * 0.044715) * square)
+        pre_grad = hidden_grad_ref[:, cols] * slope
+        b_in_grad_ref[:, cols] = jnp.sum(pre_grad, axis=0, keepdims=True)
+        pre_grad = pre_grad.astype(LINK)
+        hidden_ref[:, cols] = hidden
+        pre_grad_ref[:, cols] = pre_grad
+        grad_in_ref[:, cols] = dot(act, pre_grad, ((0,), (0,)))
+        grad_out_ref[:, cols] = dot(branch_grad, hidden, ((0,), (0,)))
+    first = lax.axis_index("dp") == 0
+
+    @pl.when(first)
+    def _():
+        keep_ref[...] = grad_in_ref[...]
+        send_ref[...] = grad_out_ref[...].astype(LINK)
+
+    @pl.when(jnp.logical_not(first))
+    def _():
+        keep_ref[...] = grad_out_ref[...]
+        send_ref[...] = grad_in_ref[...].astype(LINK)
+
+
+def norm_back_kernel(
+    pre_grad_ref, w_in_ref, normed_ref, inv_std_ref, gain_ref, conv_grad_ref, sums_ref
+):
+    act_grad = dot(pre_grad_ref[...], w_in_ref[...], ((1,), (1,)))
+    normed = normed_ref[...]
+    scaled = act_grad * gain_ref[...]
+    conv_grad = inv_std_ref[...][:, :1] * (
+        scaled
+        - jnp.mean(scaled, axis=1, keepdims=True)
+        - normed * jnp.mean(scaled * normed, axis=1, keepdims=True)
+    )
+    conv_grad_ref[...] = conv_grad
+    for i, value in enumerate((conv_grad, act_grad * normed, act_grad)):
+        sums_ref[i : i + 1, :] = jnp.sum(value, axis=0, keepdims=True)
+
+
+def lat_send_kernel(tw, keep_ref, other_ref, conv_grad_ref, send_ref, mine_ref):
+    rows = mine_ref.shape[0]
+    cells, channels = conv_grad_ref.shape
+    lat = lax.axis_index("lat")
+    mine = pl.ds(pl.multiple_of(lat * rows, 8), rows)
+    theirs = pl.ds(pl.multiple_of((1 - lat) * rows, 8), rows)
+    mine_ref[...] = keep_ref[mine, :] + other_ref[mine, :].astype(F32)
+    send_ref[:rows, :] = (keep_ref[theirs, :] + other_ref[theirs, :].astype(F32)).astype(LINK)
+    for r in range(3):
+        tail = conv_grad_ref[pl.ds(cells - (3 - r) * tw, tw), :]
+        head = conv_grad_ref[pl.ds(r * tw, tw), :]
+        send_ref[pl.ds(rows, tw), pl.ds(r * SLOT, channels)] = jnp.where(
+            lat == 0, tail, head
+        ).astype(LINK)
+
+
+def kernel_grad_kernel(
+    tile_h, tw, start_ref, lat_ref, near_ref, far_ref, conv_grad_ref, sums_ref, b_in_grad_ref,
+    hidden_ref, w_out_ref, b_out_ref, full_ref, cot_ref, scale_ref,
+    send_ref, block_out_hbm, out_ref, padded_ref, shifts_ref, block_out_ref, sems,
+):
+    channels = conv_grad_ref.shape[1]
+    branch = dot(hidden_ref[...], w_out_ref[...], ((1,), (1,))) + b_out_ref[...]
+    full = full_ref[...]
+    out_grad = cot_ref[...].astype(F32) * full
+    scale = scale_ref[...]
+    block_out_ref[...] = (full * (start_ref[...].astype(F32) + scale * branch)).astype(LINK)
+    write = copies(((block_out_ref, block_out_hbm),), sems)
+    places = tap_slots(49 + 5)
+    out_ref[...] = jnp.zeros(out_ref.shape, F32)
+    sums = [sums_ref[i : i + 1, :] for i in range(3)] + [
+        jnp.sum(value, axis=0, keepdims=True) for value in (out_grad * scale, out_grad * branch)
+    ]
+    for i, value in enumerate(sums):
+        row, lane = places[49 + i]
+        out_ref[row : row + 1, pl.ds(lane, channels)] = value
+    top, bottom = lat_rows(lambda r: lat_ref[pl.ds(r * tw, tw), :], tw)
+    fill_center(
+        padded_ref, lambda h: start_ref[pl.ds(h * tw, tw), :].astype(F32), tile_h, tw, top, bottom
+    )
+    read_edges(padded_ref, tw, channels, near_ref, far_ref, 0)
+    shift_all(padded_ref, shifts_ref, tile_h, tw)
+    for q in range(7):
+
+        def step(h, totals):
+            base = pl.multiple_of(h * tw, 8)
+            grad = conv_grad_ref[pl.ds(base, tw), :]
+            rows = shifts_ref[q, pl.ds(base, 7 * tw), :]
+            new = []
+            for r in range(7):
+                product = grad * rows[r * tw : (r + 1) * tw]
+                new.append(totals[r] + sum(product[8 * p : 8 * p + 8] for p in range(tw // 8)))
+            return tuple(new)
+
+        totals = lax.fori_loop(
+            0, tile_h, step, tuple(jnp.zeros((8, channels), F32) for _ in range(7))
+        )
+        for r in range(7):
+            row, lane = places[r * 7 + q]
+            out_ref[row : row + 1, pl.ds(lane, channels)] = jnp.sum(
+                totals[r], axis=0, keepdims=True
+            )
+    out_ref[out_ref.shape[0] - 1 :, :] = b_in_grad_ref[...]
+    send_ref[...] = out_ref[...].astype(LINK)
+    write[0].wait()
+
+
+def lon_send_kernel(
+    tile_h, tw, mine_ref, lat_ref, conv_grad_ref, small_ref, small_other_ref,
+    near_ref, across_ref, far_ref, own_ref, total_ref, smalls_ref, padded_ref,
+):
+    rows = mine_ref.shape[0]
+    chunk = rows // 4
+    total_ref[...] = mine_ref[...] + lat_ref[:rows, :].astype(F32)
+    smalls_ref[...] = small_ref[...].astype(F32) + small_other_ref[...].astype(F32)
+    lon = lax.axis_index("lon")
+
+    def fill(ref, index):
+        ref[:chunk, :] = total_ref[pl.ds(pl.multiple_of(index * chunk, 8), chunk), :].astype(
+            ref.dtype
+        )
+        ref[chunk : chunk + 8, :] = smalls_ref[pl.ds(pl.multiple_of(index * 8, 8), 8), :].astype(
+            ref.dtype
+        )
+
+    fill(near_ref, lon ^ 1)
+    fill(across_ref, lon ^ 2)
+    fill(far_ref, lon ^ 3)
+    fill(own_ref, lon)
+    channels = conv_grad_ref.shape[1]
+    top, bottom = lat_rows(lambda r: lat_ref[pl.ds(rows, tw), pl.ds(r * SLOT, channels)], tw)
+    fill_center(
+        padded_ref, lambda h: conv_grad_ref[pl.ds(h * tw, tw), :], tile_h, tw, top, bottom
+    )
+    write_edges(padded_ref, tw, channels, near_ref, far_ref, chunk + 8)
+
+
+def reduce_kernel(factor, own_ref, near_ref, across_ref, far_ref, out_ref):
+    rows = own_ref.shape[0]
+    total = own_ref[...] + near_ref[:rows, :].astype(F32)
+    total = total + across_ref[...].astype(F32) + far_ref[:rows, :].astype(F32)
+    out_ref[...] = (total * factor).astype(LINK)
+
+
+def field_grad_kernel(
+    tile_h, tw, row, rows, conv_grad_ref, lat_ref, near_ref, far_ref, kernel_ref, full_ref, cot_ref,
+    out_hbm, padded_ref, shifts_ref, conv_ref, result_ref, sems,
+):
+    channels = conv_grad_ref.shape[1]
+    top, bottom = lat_rows(lambda r: lat_ref[pl.ds(rows, tw), pl.ds(r * SLOT, channels)], tw)
+    fill_center(
+        padded_ref, lambda h: conv_grad_ref[pl.ds(h * tw, tw), :], tile_h, tw, top, bottom
+    )
+    read_edges(padded_ref, tw, channels, near_ref, far_ref, row)
+    shift_all(padded_ref, shifts_ref, tile_h, tw)
+    convolve(shifts_ref, kernel_ref, conv_ref, tile_h, tw, True)
+    full = full_ref[...]
+    result_ref[...] = (full * (cot_ref[...].astype(F32) * full + conv_ref[...])).astype(LINK)
+    copies(((result_ref, out_hbm),), sems)[0].wait()
+
+
+def lon_gather_kernel(own_ref, near_ref, across_ref, far_ref, send_ref, mine_ref):
+    chunk = own_ref.shape[0] - 8
+    rows = 4 * chunk
+    lon = lax.axis_index("lon")
+    for step, ref in enumerate((own_ref, near_ref, across_ref, far_ref)):
+        index = lon ^ step
+        send_ref[pl.ds(pl.multiple_of(index * chunk, 8), chunk), :] = ref[:chunk, :]
+        send_ref[pl.ds(pl.multiple_of(rows + index * 8, 8), 8), :] = ref[chunk:, :]
+    mine_ref[...] = send_ref[:rows, :]
+
+
+def unpack_kernel(
+    own_ref, lat_ref, dp_own_ref, dp_lat_ref,
+    grad_in_ref, grad_out_ref, kernel_ref, bias_ref, gain_ref, ln_bias_ref, b_in_ref, b_out_ref, scale_ref,
+    small_ref,
+):
+    rows = dp_own_ref.shape[0]
+    channels = kernel_ref.shape[2]
+    lat = lax.axis_index("lat")
+    first = lax.axis_index("dp") == 0
+    here = pl.ds(pl.multiple_of(lat * rows, 8), rows)
+    there = pl.ds(pl.multiple_of((1 - lat) * rows, 8), rows)
+
+    def put(mine_ref, other_ref):
+        mine_ref[here, :] = own_ref[:rows, :].astype(F32)
+        mine_ref[there, :] = lat_ref[:rows, :].astype(F32)
+        other_ref[here, :] = dp_own_ref[...].astype(F32)
+        other_ref[there, :] = dp_lat_ref[:rows, :].astype(F32)
+
+    @pl.when(first)
+    def _():
+        put(grad_in_ref, grad_out_ref)
+
+    @pl.when(jnp.logical_not(first))
+    def _():
+        put(grad_out_ref, grad_in_ref)
+
+    small_ref[...] = own_ref[rows:, :].astype(F32) + lat_ref[rows:, :].astype(F32)
+    places = tap_slots(54)
+    for i in range(49):
+        row, lane = places[i]
+        kernel_ref[i // 7, i % 7 : i % 7 + 1, :] = small_ref[row : row + 1, pl.ds(lane, channels)]
+    for i, ref in enumerate((bias_ref, gain_ref, ln_bias_ref, b_out_ref, scale_ref)):
+        row, lane = places[49 + i]
+        ref[...] = small_ref[row : row + 1, pl.ds(lane, channels)]
+    b_in_ref[...] = small_ref[small_ref.shape[0] - 1, :]
+
+
+def swap(axis, step):
+    return [(i, i ^ step) for i in range(lax.axis_size(axis))]
+
+
+def fast_body(
+    fields, cotangent, ocean_mask, dw_kernel, dw_bias, ln_gain, ln_bias, w_in, b_in, w_out, b_out,
+    layer_scale,
+):
+    snapshots, tile_h, tw, channels = fields.shape
+    cells = tile_h * tw
+    hid = w_in.shape[1]
+    fields2 = fields.reshape(cells, channels)
+    cot2 = cotangent.reshape(cells, channels)
+    row = lambda vector: vector.reshape(1, -1)
+    w_out_t = w_out.T
+    padded = pltpu.VMEM((-(-channels // 128), PAD_ROWS * STRIDE, 128), F32)
+    shifts_shape = (7, (tile_h + 6) * tw, channels)
+    tile = (cells, channels)
+
+    sems = lambda count: pltpu.SemaphoreType.DMA((count,))
+    start, edge, full = call(
+        functools.partial(prepare_kernel, tw),
+        [(tile, LINK), ((3 * tw, channels), LINK), (tile, F32)],
+        (fields2, ocean_mask),
+        scratch=[pltpu.VMEM(tile, LINK), pltpu.VMEM(ocean_mask.shape, jnp.int32), sems(2)],
+        hbm=(0, 1),
+    )
+    lat_in = lax.ppermute(edge, "lat", swap("lat", 1))
+    held = (
+        cot2, row(layer_scale), w_out_t, dw_kernel, row(dw_bias), row(ln_gain), row(ln_bias), w_in, b_in,
+        row(b_out),
+    )
+    loaded = call(
+        load_kernel,
+        [(array.shape, array.dtype) for array in held] + [(tile, LINK), ((cells, hid), F32)],
+        (full, *held),
+        2 * cells * channels * hid,
+        scratch=[sems(len(held))],
+        hbm=range(1, 1 + len(held)),
+    )
+    cot2, scale, w_out_v, taps, bias, gain, ln_b, w_in_v, b_in_v, b_out_v = loaded[: len(held)]
+    branch_grad, hidden_grad = loaded[len(held) :]
+    near, far = call(
+        functools.partial(edges_kernel, tile_h, tw),
+        [((PAD_ROWS, 3 * SLOT), LINK)] * 2,
+        (start, lat_in, bias),
+        scratch=[padded],
+    )
+    near_in = lax.ppermute(near, "lon", swap("lon", 1))
+    far_in = lax.ppermute(far, "lon", swap("lon", 3))
+    split = (-(-channels // 128), cells, 128)
+    (inner,) = call(
+        functools.partial(inner_conv_kernel, tile_h, tw),
+        [(split, F32)],
+        (start, lat_in, taps, bias),
+        100 * cells * channels,
+        scratch=[padded, pltpu.VMEM(shifts_shape, F32), pltpu.VMEM(tile, F32)],
+    )
+    send, keep, normed, inv_std, hidden, pre_grad, b_in_grad = call(
+        functools.partial(main_kernel, tile_h, tw),
+        [
+            ((channels, hid), LINK),
+            ((channels, hid), F32),
+            (tile, F32),
+            ((cells, 128), F32),
+            ((cells, hid), LINK),
+            ((cells, hid), LINK),
+            ((1, hid), F32),
+        ],
+        (inner, near_in, far_in, taps, gain, ln_b, branch_grad, hidden_grad, w_in_v, b_in_v),
+        6 * cells * channels * hid,
+        scratch=[
+            pltpu.VMEM(split, F32),
+            pltpu.VMEM((channels, hid), F32),
+            pltpu.VMEM((channels, hid), F32),
+        ],
+    )
+    other = lax.ppermute(send, "dp", swap("dp", 1))
+    conv_grad, sums = call(
+        norm_back_kernel,
+        [(tile, F32), ((3, channels), F32)],
+        (pre_grad, w_in_v, normed, inv_std, gain),
+        2 * cells * channels * hid,
+    )
+    half = channels // 2
+    lat_send, mine = call(
+        functools.partial(lat_send_kernel, tw),
+        [((half + tw, hid), LINK), ((half, hid), F32)],
+        (keep, other, conv_grad),
+    )
+    lat_got = lax.ppermute(lat_send, "lat", swap("lat", 1))
+    small_rows = 32
+    small, block_out = call(
+        functools.partial(kernel_grad_kernel, tile_h, tw),
+        [((small_rows, hid), LINK), (tile, LINK)],
+        (
+            start, lat_in, near_in, far_in, conv_grad, sums, b_in_grad, hidden, w_out_v, b_out_v, full,
+            cot2, scale,
+        ),
+        100 * cells * channels + 2 * cells * channels * hid,
+        scratch=[
+            pltpu.VMEM((small_rows, hid), F32),
+            padded,
+            pltpu.VMEM(shifts_shape, F32),
+            pltpu.VMEM(tile, LINK),
+            sems(1),
+        ],
+        hbm_out=(1,),
+    )
+    small_other = lax.ppermute(small, "dp", swap("dp", 1))
+    chunk = half // 4
+    part = chunk + 8
+    near, across, far, own = call(
+        functools.partial(lon_send_kernel, tile_h, tw),
+        [
+            ((part + PAD_ROWS, hid), LINK),
+            ((part, hid), LINK),
+            ((part + PAD_ROWS, hid), LINK),
+            ((part, hid), F32),
+        ],
+        (mine, lat_got, conv_grad, small, small_other),
+        scratch=[pltpu.VMEM((half, hid), F32), pltpu.VMEM((small_rows, hid), F32), padded],
+    )
+    near_got = lax.ppermute(near, "lon", swap("lon", 1))
+    across_got = lax.ppermute(across, "lon", swap("lon", 2))
+    far_got = lax.ppermute(far, "lon", swap("lon", 3))
+    members = lax.axis_size("lon") * lax.axis_size("lat") * lax.axis_size("dp")
+    factor = 1.0 / math.sqrt(snapshots * cells * members)
+    (reduced,) = call(
+        functools.partial(reduce_kernel, factor),
+        [((part, hid), LINK)],
+        (own, near_got, across_got, far_got),
+    )
+    gathered = [lax.ppermute(reduced, "lon", swap("lon", step)) for step in (1, 2, 3)]
+    (field_grad,) = call(
+        functools.partial(field_grad_kernel, tile_h, tw, part, half),
+        [(tile, LINK)],
+        (conv_grad, lat_got, near_got, far_got, taps, full, cot2),
+        100 * cells * channels,
+        scratch=[
+            padded, pltpu.VMEM(shifts_shape, F32), pltpu.VMEM(tile, F32), pltpu.VMEM(tile, LINK), sems(1),
+        ],
+        hbm_out=(0,),
+    )
+    send, mine = call(
+        lon_gather_kernel,
+        [((half + small_rows, hid), LINK), ((half, hid), LINK)],
+        (reduced, *gathered),
+    )
+    lat_got = lax.ppermute(send, "lat", swap("lat", 1))
+    dp_own = lax.ppermute(mine, "dp", swap("dp", 1))
+    lat_got, field_grad = lax.optimization_barrier((lat_got, field_grad))
+    dp_lat = lax.ppermute(lat_got, "dp", swap("dp", 1))
+    vector = ((1, channels), F32)
+    outs = call(
+        unpack_kernel,
+        [
+            ((channels, hid), F32),
+            ((channels, hid), F32),
+            (dw_kernel.shape, F32),
+            vector, vector, vector,
+            ((hid,), F32),
+            vector, vector,
+        ],
+        (send, lat_got, dp_own, dp_lat),
+        scratch=[pltpu.VMEM((small_rows, hid), F32)],
+    )
+    grad_in, grad_out, grad_kernel, bias_g, gain_g, ln_b_g, b_in_g, b_out_g, scale_g = outs
+    return (
+        block_out.reshape(fields.shape),
+        field_grad.reshape(fields.shape),
+        grad_kernel,
+        bias_g.reshape(-1),
+        gain_g.reshape(-1),
+        ln_b_g.reshape(-1),
+        grad_in,
+        b_in_g,
+        grad_out.T,
+        b_out_g.reshape(-1),
+        scale_g.reshape(-1),
+    )
+
+
 def solution(mesh):
+    sizes = dict(mesh.shape)
+    paired = sizes["lat"] == 2 and sizes["lon"] == 4 and sizes["dp"] == 2
     return jax.shard_map(
-        body,
+        fast_body if paired else body,
         mesh=mesh,
         in_specs=(
             P(("groups", "dp"), "lat", "lon", None),

time: 71.4 us -> 53.2 us (0.75)
  other arithmetic: 14.1 us -> 0 us
  Pallas kernels: 0 us -> 11.8 us
  starting transfers between devices: 21.8 us -> 17 us
  matrix products: 4.41 us -> 0 us
  local copies, waits for them, and re-layouts: 8.58 us -> 5.1 us
  between operations: 2.47 us -> 0.82 us
  waiting for transfers between devices: 19.7 us -> 18.2 us
    pallas_call x0 -> x13, Pallas kernels: none -> 11.8 us  [call(): pl.pallas_call(kernel, out_shape=tuple((jax.ShapeDtypeStruct(s, d) for s,...]
    reduce_sum x8 -> x0, other arithmetic: 6.65 us -> none  [the longest x1 2.49 us: body(): center = jnp.mean(conv_out, axis=-1, keepdims=True)]
    ppermute x16 -> x15, starting transfers between devices: 21.8 us -> 17 us  [the longest x3 4.45 us: fast_body(): lax.ppermute(reduced, 'lon', swap('lon', step))]
    convert_element_type x5 -> x0, other arithmetic: 4.44 us -> none  [the longest x1 3.3 us: body(): field_grad = (ocean * (out_grad + depthwise_back(grad_padded, dw_kernel,...]
    dot_general x6 -> x0, matrix products: 4.41 us -> none  [the longest x1 1.27 us: mlp_pass(): hidden_grad = jnp.dot(branch_b, w_out.T, preferred_element_type=jnp.float32)]
    slice x8 -> x0, local copies, waits for them, and re-layouts: 4.28 us -> none  [the longest x3 3.48 us: depthwise(): kernel[row_off, col_off]]
    unnamed x194 -> x24, local copies, waits for them, and re-layouts: 0.86 us -> 5.1 us
    reshape x5 -> x0, local copies, waits for them, and re-layouts: 1.49 us -> none  [the longest x1 0.67 us: body(): small[taps + 5:].reshape(hid)]
  transfers between devices with their start and end apart: 16 -> 15, of which waited for: 9 -> 9; matrix products, arithmetic and copies ran while one was open for 10% -> 0% of each run, Pallas kernels for 0% -> 15%
where the time goes in v2:
time: 53.2 us; the launch traced here: 52.9 us
  waiting for transfers between devices  18.2 us (34%)
  starting transfers between devices  17 us (32%)
  Pallas kernels  11.8 us (22%)
  local copies, waits for them, and re-layouts  5.1 us (10%)
  between operations  0.82 us (2%)
    pallas_call x13, Pallas kernels, call(): pl.pallas_call(kernel, out_shape=tuple((jax.ShapeDtypeStruct(s, d) for s,...  11.8 us
    ppermute x1, waiting for transfers between devices, fast_body(): across_got = lax.ppermute(across, 'lon', swap('lon', 2))  5.64 us
    unnamed x24, local copies, waits for them, and re-layouts  5.1 us
    ppermute x3, starting transfers between devices, fast_body(): lax.ppermute(reduced, 'lon', swap('lon', step))  4.45 us
    ppermute x3, waiting for transfers between devices, fast_body(): lax.ppermute(reduced, 'lon', swap('lon', step))  3.08 us
    ppermute x1, starting transfers between devices, fast_body(): lat_in = lax.ppermute(edge, 'lat', swap('lat', 1))  3.03 us
    ppermute x1, waiting for transfers between devices, fast_body(): lat_got = lax.ppermute(send, 'lat', swap('lat', 1))  2.57 us
    ppermute x1, starting transfers between devices, fast_body(): far_got = lax.ppermute(far, 'lon', swap('lon', 3))  2.54 us
  transfers between devices with their start and end apart: 15, of which 9 were waited for; matrix products, arithmetic and copies ran while one was open for 0% of the time, Pallas kernels for 15%

profile of v2, /device:TPU:0, one launch (start us, length us, event | category | flops | bytes accessed | tf_op | source)
XLA Modules:
  0.0 52.9 jit_solution(7182729870165233197)
XLA Ops:
  0.7 0.9 %copy-done.3 = bf16[1,16,16,192]{3,2,1,0:T(8,128)(2,1)S(1)} copy-done((bf16[1,16,16,192]{3,2,1,0:T(8,128)(2,1)S(1)}, bf16[1,16,16,192]{3,2,1,0:T(8,128)(2,1)}, u32[]{:S(2)}) %copy-start.3) | copy-done | bytes 98328
  1.6 0.7 %copy-done.5 = s32[16,16]{1,0:T(8,128)S(1)} copy-done((s32[16,16]{1,0:T(8,128)S(1)}, s32[16,16]{1,0:T(8,128)}, u32[]{:S(2)}) %copy-start.5) | copy-done | bytes 1048
  2.3 0.5 shard_map.203
  2.8 3.0 %collective-permute-start = (bf16[48,192]{1,0:T(8,128)(2,1)S(1)}, bf16[48,192]{1,0:T(8,128)(2,1)S(1)}, u32[]{:S(2)}, u32[]{:S(2)}) collective-permute-start(bf16[48,192]{1,0:T(8,128)(2,1)S(1)} %get-tuple-element.59), channel_id=1, source_target_pairs={{0,2},{2,0},{1,3},{3,1},{4,6},{6,4},{5,7},{7,5},{8,10},{10,8},{9,1... | collective-permute-start | bytes 55304 | tf_op jit(solution)/shard_map/ppermute | solution.py:766
  5.9 0.0 copy-start.9
  5.9 0.0 copy-start.7
  5.9 0.6 %copy-done.10 = f32[192]{0:T(256)S(1)} copy-done((f32[192]{0:T(256)S(1)}, f32[192]{0:T(256)}, u32[]{:S(2)}) %copy-start.10) | copy-done | bytes 792
  6.5 0.0 copy-done.11
  6.5 0.0 copy-done.6
  6.6 0.0 copy-done.8
  6.6 0.0 copy-done.9
  6.6 0.0 copy-done.7
  6.6 1.0 %copy-done = bf16[768,192]{0,1:T(8,128)(2,1)S(1)} copy-done((bf16[768,192]{0,1:T(8,128)(2,1)S(1)}, bf16[768,192]{0,1:T(8,128)(2,1)}, u32[]{:S(2)}) %copy-start) | copy-done | bytes 294936
  7.6 1.0 %copy-done.1 = bf16[192,768]{1,0:T(8,128)(2,1)S(1)} copy-done((bf16[192,768]{1,0:T(8,128)(2,1)S(1)}, bf16[192,768]{1,0:T(8,128)(2,1)}, u32[]{:S(2)}) %copy-start.1) | copy-done | bytes 294936
  8.5 0.8 %copy-done.4 = f32[7,7,192]{2,1,0:T(8,128)S(1)} copy-done((f32[7,7,192]{2,1,0:T(8,128)S(1)}, f32[7,7,192]{2,1,0:T(8,128)}, u32[]{:S(2)}) %copy-start.4) | copy-done | bytes 37656
  9.3 0.8 %shard_map.204 = (bf16[256,192]{1,0:T(8,128)(2,1)S(1)}, f32[1,192]{1,0:T(1,128)S(1)}, bf16[192,768]{1,0:T(8,128)(2,1)S(1)}, f32[7,7,192]{2,1,0:T(8,128)S(1)}, f3...) custom-call(f32[256,192]{1,0:T(8,128)S(1)} %get-tuple-element.60.ful, ...), custom_call_target="tpu_custom_call" | custom-call | flops 75497472 | bytes 2546688 | tf_op jit(solution)/shard_map/pallas_call | solution.py:308
  10.1 0.1 shard_map.205
  10.2 1.6 %collective-permute-start.1 = (bf16[24,768]{1,0:T(8,128)(2,1)S(1)}, bf16[24,768]{1,0:T(8,128)(2,1)S(1)}, u32[]{:S(2)}, u32[]{:S(2)}) collective-permute-start(bf16[24,768]{1,0:T(8,128)(2,1)S(1)} %get-tuple-element.62), channel_id=1, source_target_pairs={{0,4},{4,0},{8,12},{12,8},{1,5},{5,1},{9,13},{13,9},{2,6},{6,2},{1... | collective-permute-start | bytes 110600 | tf_op jit(solution)/shard_map/ppermute | solution.py:787
  11.9 2.5 %collective-permute-start.2 = (bf16[24,768]{1,0:T(8,128)(2,1)S(1)}, bf16[24,768]{1,0:T(8,128)(2,1)S(1)}, u32[]{:S(2)}, u32[]{:S(2)}) collective-permute-start(bf16[24,768]{1,0:T(8,128)(2,1)S(1)} %get-tuple-element.63), channel_id=1, source_target_pairs={{0,12},{4,8},{8,4},{12,0},{1,13},{5,9},{9,5},{13,1},{2,14},{6,10},... | collective-permute-start | bytes 110600 | tf_op jit(solution)/shard_map/ppermute | solution.py:788
  14.4 1.9 %shard_map.206.inner_ref = f32[2,256,128]{2,1,0:T(8,128)S(1)} custom-call(bf16[256,192]{1,0:T(8,128)(2,1)S(1)} %get-tuple-element.58.start_ref, bf16[48,192]{1,0:T(8,128)(2,1)S(1)} %collective-permute-done.lat_ref, f32[7,7,192]{2,1,0:T(8,128)S(1)} %get-tuple-element.64.kernel_ref, f32[1,192]{1,0:T(1,128)S(1)} %get-tuple-element.61.loaded_ref.bias_ref), custom_call_target="tpu_custom_call" | custom-call | flops 4915200 | bytes 417280 | tf_op jit(solution)/shard_map/pallas_call | solution.py:308
  16.2 0.0 collective-permute-done.1.near_ref
  16.3 1.4 %collective-permute-done.2.far_ref = bf16[24,768]{1,0:T(8,128)(2,1)S(1)} collective-permute-done((bf16[24,768]{1,0:T(8,128)(2,1)S(1)}, bf16[24,768]{1,0:T(8,128)(2,1)S(1)}, u32[]{:S(2)}, u32[]{:S(2)}) %collective-permute-start.2) | collective-permute-done | bytes 36896 | tf_op jit(solution)/shard_map/ppermute | solution.py:788
  17.6 1.5 %shard_map.207 = (bf16[192,768]{1,0:T(8,128)(2,1)S(1)}, f32[192,768]{1,0:T(8,128)S(1)}, f32[256,192]{1,0:T(8,128)S(1)}, f32[256,128]{1,0:T(8,128)S(1)}, bf16[256...) custom-call(f32[2,256,128]{2,1,0:T(8,128)S(1)} %shard_map.206.inner_ref, ...), custom_call_target="tpu_custom_call" | custom-call | flops 226492416 | bytes 3559680 | tf_op jit(solution)/shard_map/pallas_call | solution.py:308
  19.2 0.1 collective-permute-start.3
  19.2 0.5 shard_map.208
  19.7 1.1 %collective-permute-done.3.other_ref = bf16[192,768]{1,0:T(8,128)(2,1)S(1)} collective-permute-done((bf16[192,768]{1,0:T(8,128)(2,1)S(1)}, bf16[192,768]{1,0:T(8,128)(2,1)S(1)}, u32[]{:S(2)}, u32[]{:S(2)}) %collective-permute-start.3) | collective-permute-done | bytes 294944 | tf_op jit(solution)/shard_map/ppermute | solution.py:816
  20.8 0.1 shard_map.210
  20.9 0.6 %collective-permute-start.4 = (bf16[112,768]{1,0:T(8,128)(2,1)S(1)}, bf16[112,768]{1,0:T(8,128)(2,1)S(1)}, u32[]{:S(2)}, u32[]{:S(2)}) collective-permute-start(bf16[112,768]{1,0:T(8,128)(2,1)S(1)} %get-tuple-element.86), channel_id=1, source_target_pairs={{0,2},{2,0},{1,3},{3,1},{4,6},{6,4},{5,7},{7,5},{8,10},{10,8},{9,1... | collective-permute-start | bytes 516104 | tf_op jit(solution)/shard_map/ppermute | solution.py:829
  21.5 2.5 %shard_map.209 = (bf16[32,768]{1,0:T(8,128)(2,1)S(1)}, bf16[256,192]{1,0:T(8,128)(2,1)}) custom-call(bf16[256,192]{1,0:T(8,128)(2,1)S(1)} %get-tuple-element.58.start_ref, bf16[48,192]{1,0:T(8,128)(2,1)S(1)} %collective-permute-done.lat_ref, bf16[24,768]{1,0:T(8,128)(2,1)S(1)} %collective-permute-done.1.near_ref, ...), custom_call_target="tpu_custom_call" | custom-call | flops 80412672 | bytes 1524480 | tf_op jit(solution)/shard_map/pallas_call | solution.py:308
  24.0 0.1 collective-permute-start.5
  24.1 1.2 %collective-permute-done.5.small_other_ref = bf16[32,768]{1,0:T(8,128)(2,1)S(1)} collective-permute-done((bf16[32,768]{1,0:T(8,128)(2,1)S(1)}, bf16[32,768]{1,0:T(8,128)(2,1)S(1)}, u32[]{:S(2)}, u32[]{:S(2)}) %collective-permute-start.5) | collective-permute-done | bytes 49184 | tf_op jit(solution)/shard_map/ppermute | solution.py:848
  25.3 2.1 %collective-permute-done.4.lat_ref = bf16[112,768]{1,0:T(8,128)(2,1)S(1)} collective-permute-done((bf16[112,768]{1,0:T(8,128)(2,1)S(1)}, bf16[112,768]{1,0:T(8,128)(2,1)S(1)}, u32[]{:S(2)}, u32[]{:S(2)}) %collective-permute-start.4) | collective-permute-done | bytes 172064 | tf_op jit(solution)/shard_map/ppermute | solution.py:829
  27.4 0.2 shard_map.211
  27.6 0.1 collective-permute-start.6
  27.6 2.5 %collective-permute-start.8 = (bf16[56,768]{1,0:T(8,128)(2,1)S(1)}, bf16[56,768]{1,0:T(8,128)(2,1)S(1)}, u32[]{:S(2)}, u32[]{:S(2)}) collective-permute-start(bf16[56,768]{1,0:T(8,128)(2,1)S(1)} %get-tuple-element.91), channel_id=1, source_target_pairs={{0,12},{4,8},{8,4},{12,0},{1,13},{5,9},{9,5},{13,1},{2,14},{6,10},... | collective-permute-start | bytes 258056 | tf_op jit(solution)/shard_map/ppermute | solution.py:864
  30.2 0.9 %collective-permute-start.7 = (bf16[32,768]{1,0:T(8,128)(2,1)S(1)}, bf16[32,768]{1,0:T(8,128)(2,1)S(1)}, u32[]{:S(2)}, u32[]{:S(2)}) collective-permute-start(bf16[32,768]{1,0:T(8,128)(2,1)S(1)} %get-tuple-element.90), channel_id=1, source_target_pairs={{0,8},{4,12},{8,0},{12,4},{1,9},{5,13},{9,1},{13,5},{2,10},{6,14},... | collective-permute-start | bytes 147464 | tf_op jit(solution)/shard_map/ppermute | solution.py:863
  31.1 5.6 %collective-permute-done.7.across_ref = bf16[32,768]{1,0:T(8,128)(2,1)S(1)} collective-permute-done((bf16[32,768]{1,0:T(8,128)(2,1)S(1)}, bf16[32,768]{1,0:T(8,128)(2,1)S(1)}, u32[]{:S(2)}, u32[]{:S(2)}) %collective-permute-start.7) | collective-permute-done | bytes 49184 | tf_op jit(solution)/shard_map/ppermute | solution.py:863
  36.8 2.3 %collective-permute-start.11 = (bf16[32,768]{1,0:T(8,128)(2,1)S(1)}, bf16[32,768]{1,0:T(8,128)(2,1)S(1)}, u32[]{:S(2)}, u32[]{:S(2)}) collective-permute-start(bf16[32,768]{1,0:T(8,128)(2,1)S(1)} %shard_map.212.own_ref), channel_id=1, source_target_pairs={{0,12},{4,8},{8,4},{12,0},{1,13},{5,9},{9,5},{13,1},{2,14},{6,10},... | collective-permute-start | bytes 147464 | tf_op jit(solution)/shard_map/ppermute | solution.py:872
  39.1 0.0 collective-permute-start.10
  39.1 2.2 %collective-permute-start.9 = (bf16[32,768]{1,0:T(8,128)(2,1)S(1)}, bf16[32,768]{1,0:T(8,128)(2,1)S(1)}, u32[]{:S(2)}, u32[]{:S(2)}) collective-permute-start(bf16[32,768]{1,0:T(8,128)(2,1)S(1)} %shard_map.212.own_ref), channel_id=1, source_target_pairs={{0,4},{4,0},{8,12},{12,8},{1,5},{5,1},{9,13},{13,9},{2,6},{6,2},{1... | collective-permute-start | bytes 147464 | tf_op jit(solution)/shard_map/ppermute | solution.py:872
  41.2 1.8 %collective-permute-done.11.far_ref = bf16[32,768]{1,0:T(8,128)(2,1)S(1)} collective-permute-done((bf16[32,768]{1,0:T(8,128)(2,1)S(1)}, bf16[32,768]{1,0:T(8,128)(2,1)S(1)}, u32[]{:S(2)}, u32[]{:S(2)}) %collective-permute-start.11) | collective-permute-done | bytes 49184 | tf_op jit(solution)/shard_map/ppermute | solution.py:872
  43.1 1.2 %collective-permute-done.10.across_ref = bf16[32,768]{1,0:T(8,128)(2,1)S(1)} collective-permute-done((bf16[32,768]{1,0:T(8,128)(2,1)S(1)}, bf16[32,768]{1,0:T(8,128)(2,1)S(1)}, u32[]{:S(2)}, u32[]{:S(2)}) %collective-permute-start.10) | collective-permute-done | bytes 49184 | tf_op jit(solution)/shard_map/ppermute | solution.py:872
  44.4 0.6 %collective-permute-start.12 = (bf16[128,768]{1,0:T(8,128)(2,1)S(1)}, bf16[128,768]{1,0:T(8,128)(2,1)S(1)}, u32[]{:S(2)}, u32[]{:S(2)}) collective-permute-start(bf16[128,768]{1,0:T(8,128)(2,1)S(1)} %get-tuple-element.92.own_ref), channel_id=1, source_target_pairs={{0,2},{2,0},{1,3},{3,1},{4,6},{6,4},{5,7},{7,5},{8,10},{10,8},{9,1... | collective-permute-start | bytes 589832 | tf_op jit(solution)/shard_map/ppermute | solution.py:888
  45.0 2.6 %shard_map.214 = bf16[256,192]{1,0:T(8,128)(2,1)} custom-call(f32[256,192]{1,0:T(8,128)S(1)} %get-tuple-element.74.conv_grad_ref, bf16[112,768]{1,0:T(8,128)(2,1)S(1)} %collective-permute-done.4.lat_ref, bf16[56,768]{1,0:T(8,128)(2,1)S(1)} %collective-permute-done.6.near_ref, bf16[56,768]{1,0:T(8,128)(2,1)S(1)} %collective-permute-done.8.far_ref, ...), custom_call_target="tpu_custom_call" | custom-call | flops 4915200 | bytes 971520 | tf_op jit(solution)/shard_map/pallas_call | solution.py:308
  47.5 2.6 %collective-permute-done.12.lat_ref = bf16[128,768]{1,0:T(8,128)(2,1)S(1)} collective-permute-done((bf16[128,768]{1,0:T(8,128)(2,1)S(1)}, bf16[128,768]{1,0:T(8,128)(2,1)S(1)}, u32[]{:S(2)}, u32[]{:S(2)}) %collective-permute-start.12) | collective-permute-done | bytes 196640 | tf_op jit(solution)/shard_map/ppermute | solution.py:888
  50.1 0.5 collective-permute-start.13
  50.6 1.1 %collective-permute-done.13.dp_own_ref = bf16[96,768]{1,0:T(8,128)(2,1)S(1)} collective-permute-done((bf16[96,768]{1,0:T(8,128)(2,1)S(1)}, bf16[96,768]{1,0:T(8,128)(2,1)S(1)}, u32[]{:S(2)}, u32[]{:S(2)}) %collective-permute-start.13) | collective-permute-done | bytes 147488 | tf_op jit(solution)/shard_map/ppermute | solution.py:889
  51.8 1.1 %shard_map.215 = (f32[192,768]{1,0:T(8,128)}, f32[192,768]{1,0:T(8,128)}, f32[7,7,192]{2,1,0:T(8,128)}, f32[1,192]{1,0:T(1,128)}, f32[1,192]{1,0:T(1,128)}, /*in...) custom-call(bf16[128,768]{1,0:T(8,128)(2,1)S(1)} %get-tuple-element.92.own_ref, ...), custom_call_target="tpu_custom_call" | custom-call | bytes 1961472 | tf_op jit(solution)/shard_map/pallas_call | solution.py:308
  (19 shorter events, 0.1 us)
Async XLA Ops:
  0.6 5.2 %copy-start.2 = (bf16[1,16,16,192]{3,2,1,0:T(8,128)(2,1)S(1)}, bf16[1,16,16,192]{3,2,1,0:T(8,128)(2,1)}, u32[]{:S(2)}) copy-start(bf16[1,16,16,192]{3,2,1,0:T(8,128)(2,1)} %param.13) | copy-start | bytes 294916
  0.7 0.9 %copy-start.3 = (bf16[1,16,16,192]{3,2,1,0:T(8,128)(2,1)S(1)}, bf16[1,16,16,192]{3,2,1,0:T(8,128)(2,1)}, u32[]{:S(2)}) copy-start(bf16[1,16,16,192]{3,2,1,0:T(8,128)(2,1)} %param.12) | copy-start | bytes 294916
  1.6 0.7 %copy-start.5 = (s32[16,16]{1,0:T(8,128)S(1)}, s32[16,16]{1,0:T(8,128)}, u32[]{:S(2)}) copy-start(s32[16,16]{1,0:T(8,128)} %mask_hbm.1) | copy-start | bytes 3076
  2.8 7.3 %collective-permute-start = (bf16[48,192]{1,0:T(8,128)(2,1)S(1)}, bf16[48,192]{1,0:T(8,128)(2,1)S(1)}, u32[]{:S(2)}, u32[]{:S(2)}) collective-permute-start(bf16[48,192]{1,0:T(8,128)(2,1)S(1)} %get-tuple-element.59), channel_id=1, source_target_pairs={{0,2},{2,0},{1,3},{3,1},{4,6},{6,4},{5,7},{7,5},{8,10},{10,8},{9,1... | collective-permute-start | bytes 55304 | tf_op jit(solution)/shard_map/ppermute | solution.py:766
  5.8 0.7 %copy-start.10 = (f32[192]{0:T(256)S(1)}, f32[192]{0:T(256)}, u32[]{:S(2)}) copy-start(f32[192]{0:T(256)} %param.18) | copy-start | bytes 2308
  5.8 0.7 %copy-start.11 = (f32[192]{0:T(256)S(1)}, f32[192]{0:T(256)}, u32[]{:S(2)}) copy-start(f32[192]{0:T(256)} %param.22) | copy-start | bytes 2308
  5.9 0.7 %copy-start.6 = (f32[768]{0:T(1024)S(1)}, f32[768]{0:T(1024)}, u32[]{:S(2)}) copy-start(f32[768]{0:T(1024)} %refs_8_.1) | copy-start | bytes 9220
  5.9 0.7 %copy-start.8 = (f32[192]{0:T(256)S(1)}, f32[192]{0:T(256)}, u32[]{:S(2)}) copy-start(f32[192]{0:T(256)} %param.16) | copy-start | bytes 2308
  5.9 0.7 %copy-start.9 = (f32[192]{0:T(256)S(1)}, f32[192]{0:T(256)}, u32[]{:S(2)}) copy-start(f32[192]{0:T(256)} %param.17) | copy-start | bytes 2308
  5.9 0.7 %copy-start.7 = (f32[192]{0:T(256)S(1)}, f32[192]{0:T(256)}, u32[]{:S(2)}) copy-start(f32[192]{0:T(256)} %param.23) | copy-start | bytes 2308
  6.6 1.0 %copy-start = (bf16[768,192]{0,1:T(8,128)(2,1)S(1)}, bf16[768,192]{0,1:T(8,128)(2,1)}, u32[]{:S(2)}) copy-start(bf16[768,192]{0,1:T(8,128)(2,1)} %param.21) | copy-start | bytes 884740
  7.6 1.0 %copy-start.1 = (bf16[192,768]{1,0:T(8,128)(2,1)S(1)}, bf16[192,768]{1,0:T(8,128)(2,1)}, u32[]{:S(2)}) copy-start(bf16[192,768]{1,0:T(8,128)(2,1)} %refs_7_.1) | copy-start | bytes 884740
  8.5 0.8 %copy-start.4 = (f32[7,7,192]{2,1,0:T(8,128)S(1)}, f32[7,7,192]{2,1,0:T(8,128)}, u32[]{:S(2)}) copy-start(f32[7,7,192]{2,1,0:T(8,128)} %refs_3_.1) | copy-start | bytes 112900
  10.2 6.0 %collective-permute-start.1 = (bf16[24,768]{1,0:T(8,128)(2,1)S(1)}, bf16[24,768]{1,0:T(8,128)(2,1)S(1)}, u32[]{:S(2)}, u32[]{:S(2)}) collective-permute-start(bf16[24,768]{1,0:T(8,128)(2,1)S(1)} %get-tuple-element.62), channel_id=1, source_target_pairs={{0,4},{4,0},{8,12},{12,8},{1,5},{5,1},{9,13},{13,9},{2,6},{6,2},{1... | collective-permute-start | bytes 110600 | tf_op jit(solution)/shard_map/ppermute | solution.py:787
  11.9 5.8 %collective-permute-start.2 = (bf16[24,768]{1,0:T(8,128)(2,1)S(1)}, bf16[24,768]{1,0:T(8,128)(2,1)S(1)}, u32[]{:S(2)}, u32[]{:S(2)}) collective-permute-start(bf16[24,768]{1,0:T(8,128)(2,1)S(1)} %get-tuple-element.63), channel_id=1, source_target_pairs={{0,12},{4,8},{8,4},{12,0},{1,13},{5,9},{9,5},{13,1},{2,14},{6,10},... | collective-permute-start | bytes 110600 | tf_op jit(solution)/shard_map/ppermute | solution.py:788
  19.2 1.6 %collective-permute-start.3 = (bf16[192,768]{1,0:T(8,128)(2,1)S(1)}, bf16[192,768]{1,0:T(8,128)(2,1)S(1)}, u32[]{:S(2)}, u32[]{:S(2)}) collective-permute-start(bf16[192,768]{1,0:T(8,128)(2,1)S(1)} %get-tuple-element.84), channel_id=1, source_target_pairs={{0,1},{1,0},{2,3},{3,2},{4,5},{5,4},{6,7},{7,6},{8,9},{9,8},{10,11... | collective-permute-start | bytes 884744 | tf_op jit(solution)/shard_map/ppermute | solution.py:816
  20.9 6.5 %collective-permute-start.4 = (bf16[112,768]{1,0:T(8,128)(2,1)S(1)}, bf16[112,768]{1,0:T(8,128)(2,1)S(1)}, u32[]{:S(2)}, u32[]{:S(2)}) collective-permute-start(bf16[112,768]{1,0:T(8,128)(2,1)S(1)} %get-tuple-element.86), channel_id=1, source_target_pairs={{0,2},{2,0},{1,3},{3,1},{4,6},{6,4},{5,7},{7,5},{8,10},{10,8},{9,1... | collective-permute-start | bytes 516104 | tf_op jit(solution)/shard_map/ppermute | solution.py:829
  24.0 1.3 %collective-permute-start.5 = (bf16[32,768]{1,0:T(8,128)(2,1)S(1)}, bf16[32,768]{1,0:T(8,128)(2,1)S(1)}, u32[]{:S(2)}, u32[]{:S(2)}) collective-permute-start(bf16[32,768]{1,0:T(8,128)(2,1)S(1)} %get-tuple-element.87.small_ref), channel_id=1, source_target_pairs={{0,1},{1,0},{2,3},{3,2},{4,5},{5,4},{6,7},{7,6},{8,9},{9,8},{10,11... | collective-permute-start | bytes 147464 | tf_op jit(solution)/shard_map/ppermute | solution.py:848
  27.6 9.2 %collective-permute-start.6 = (bf16[56,768]{1,0:T(8,128)(2,1)S(1)}, bf16[56,768]{1,0:T(8,128)(2,1)S(1)}, u32[]{:S(2)}, u32[]{:S(2)}) collective-permute-start(bf16[56,768]{1,0:T(8,128)(2,1)S(1)} %get-tuple-element.89), channel_id=1, source_target_pairs={{0,4},{4,0},{8,12},{12,8},{1,5},{5,1},{9,13},{13,9},{2,6},{6,2},{1... | collective-permute-start | bytes 258056 | tf_op jit(solution)/shard_map/ppermute | solution.py:862
  27.6 9.1 %collective-permute-start.8 = (bf16[56,768]{1,0:T(8,128)(2,1)S(1)}, bf16[56,768]{1,0:T(8,128)(2,1)S(1)}, u32[]{:S(2)}, u32[]{:S(2)}) collective-permute-start(bf16[56,768]{1,0:T(8,128)(2,1)S(1)} %get-tuple-element.91), channel_id=1, source_target_pairs={{0,12},{4,8},{8,4},{12,0},{1,13},{5,9},{9,5},{13,1},{2,14},{6,10},... | collective-permute-start | bytes 258056 | tf_op jit(solution)/shard_map/ppermute | solution.py:864
  30.2 6.6 %collective-permute-start.7 = (bf16[32,768]{1,0:T(8,128)(2,1)S(1)}, bf16[32,768]{1,0:T(8,128)(2,1)S(1)}, u32[]{:S(2)}, u32[]{:S(2)}) collective-permute-start(bf16[32,768]{1,0:T(8,128)(2,1)S(1)} %get-tuple-element.90), channel_id=1, source_target_pairs={{0,8},{4,12},{8,0},{12,4},{1,9},{5,13},{9,1},{13,5},{2,10},{6,14},... | collective-permute-start | bytes 147464 | tf_op jit(solution)/shard_map/ppermute | solution.py:863
  36.8 6.3 %collective-permute-start.11 = (bf16[32,768]{1,0:T(8,128)(2,1)S(1)}, bf16[32,768]{1,0:T(8,128)(2,1)S(1)}, u32[]{:S(2)}, u32[]{:S(2)}) collective-permute-start(bf16[32,768]{1,0:T(8,128)(2,1)S(1)} %shard_map.212.own_ref), channel_id=1, source_target_pairs={{0,12},{4,8},{8,4},{12,0},{1,13},{5,9},{9,5},{13,1},{2,14},{6,10},... | collective-permute-start | bytes 147464 | tf_op jit(solution)/shard_map/ppermute | solution.py:872
  39.1 5.3 %collective-permute-start.10 = (bf16[32,768]{1,0:T(8,128)(2,1)S(1)}, bf16[32,768]{1,0:T(8,128)(2,1)S(1)}, u32[]{:S(2)}, u32[]{:S(2)}) collective-permute-start(bf16[32,768]{1,0:T(8,128)(2,1)S(1)} %shard_map.212.own_ref), channel_id=1, source_target_pairs={{0,8},{4,12},{8,0},{12,4},{1,9},{5,13},{9,1},{13,5},{2,10},{6,14},... | collective-permute-start | bytes 147464 | tf_op jit(solution)/shard_map/ppermute | solution.py:872
  39.1 5.3 %collective-permute-start.9 = (bf16[32,768]{1,0:T(8,128)(2,1)S(1)}, bf16[32,768]{1,0:T(8,128)(2,1)S(1)}, u32[]{:S(2)}, u32[]{:S(2)}) collective-permute-start(bf16[32,768]{1,0:T(8,128)(2,1)S(1)} %shard_map.212.own_ref), channel_id=1, source_target_pairs={{0,4},{4,0},{8,12},{12,8},{1,5},{5,1},{9,13},{13,9},{2,6},{6,2},{1... | collective-permute-start | bytes 147464 | tf_op jit(solution)/shard_map/ppermute | solution.py:872
  44.4 5.7 %collective-permute-start.12 = (bf16[128,768]{1,0:T(8,128)(2,1)S(1)}, bf16[128,768]{1,0:T(8,128)(2,1)S(1)}, u32[]{:S(2)}, u32[]{:S(2)}) collective-permute-start(bf16[128,768]{1,0:T(8,128)(2,1)S(1)} %get-tuple-element.92.own_ref), channel_id=1, source_target_pairs={{0,2},{2,0},{1,3},{3,1},{4,6},{6,4},{5,7},{7,5},{8,10},{10,8},{9,1... | collective-permute-start | bytes 589832 | tf_op jit(solution)/shard_map/ppermute | solution.py:888
  50.1 1.7 %collective-permute-start.14 = (bf16[128,768]{1,0:T(8,128)(2,1)S(1)}, bf16[128,768]{1,0:T(8,128)(2,1)S(1)}, u32[]{:S(2)}, u32[]{:S(2)}) collective-permute-start(bf16[128,768]{1,0:T(8,128)(2,1)S(1)} %collective-permute-done.12.lat_ref), channel_id=1, source_target_pairs={{0,1},{1,0},{2,3},{3,2},{4,5},{5,4},{6,7},{7,6},{8,9},{9,8},{10,11... | collective-permute-start | bytes 589832 | tf_op jit(solution)/shard_map/ppermute | solution.py:891
  50.1 1.6 %collective-permute-start.13 = (bf16[96,768]{1,0:T(8,128)(2,1)S(1)}, bf16[96,768]{1,0:T(8,128)(2,1)S(1)}, u32[]{:S(2)}, u32[]{:S(2)}) collective-permute-start(bf16[96,768]{1,0:T(8,128)(2,1)S(1)} %get-tuple-element.95), channel_id=1, source_target_pairs={{0,1},{1,0},{2,3},{3,2},{4,5},{5,4},{6,7},{7,6},{8,9},{9,8},{10,11... | collective-permute-start | bytes 442376 | tf_op jit(solution)/shard_map/ppermute | solution.py:889

commit v3 on v2

--- a/solution.py
+++ b/solution.py
@@ -305,6 +305,9 @@
     moved = sum(a.size * a.dtype.itemsize for a in args) + sum(
         math.prod(s) * jnp.dtype(d).itemsize for s, d in outs
     )
+    args = [
+        pltpu.with_memory_space_constraint(a, pltpu.HBM) if i in hbm else a for i, a in enumerate(args)
+    ]
     return pl.pallas_call(
         kernel,
         out_shape=tuple(jax.ShapeDtypeStruct(s, d) for s, d in outs),

time: 53.2 us -> 50.1 us (0.942)
  local copies, waits for them, and re-layouts: 5.1 us -> 0 us
  starting transfers between devices: 17 us -> 19.4 us
  waiting for transfers between devices: 18.2 us -> 16.7 us
  Pallas kernels: 11.8 us -> 12.9 us
    unnamed x24 -> x0, local copies, waits for them, and re-layouts: 5.1 us -> none
    pallas_call x13, Pallas kernels: 11.8 us -> 12.9 us  [call(): pl.pallas_call(kernel, out_shape=tuple((jax.ShapeDtypeStruct(s, d) for s,...]
    ppermute x1, waiting for transfers between devices: 2.57 us -> 1.61 us  [fast_body(): lat_got = lax.ppermute(send, 'lat', swap('lat', 1))]
    ppermute x1, starting transfers between devices: 0.6 us -> 1.56 us  [fast_body(): lat_got = lax.ppermute(lat_send, 'lat', swap('lat', 1))]
    ppermute x1, starting transfers between devices: 0.6 us -> 1.56 us  [fast_body(): lat_got = lax.ppermute(send, 'lat', swap('lat', 1))]
    ppermute x1, waiting for transfers between devices: 2.07 us -> 1.11 us  [fast_body(): lat_got = lax.ppermute(lat_send, 'lat', swap('lat', 1))]
  transfers between devices with their start and end apart: 15 -> 15, of which waited for: 9 -> 10; matrix products, arithmetic and copies ran while one was open for 0% -> 0% of each run, Pallas kernels for 15% -> 18%
where the time goes in v3:
time: 50.1 us; the launch traced here: 49.8 us
  starting transfers between devices  19.4 us (39%)
  waiting for transfers between devices  16.7 us (33%)
  Pallas kernels  12.9 us (26%)
  between operations  0.76 us (2%)
    pallas_call x13, Pallas kernels, call(): pl.pallas_call(kernel, out_shape=tuple((jax.ShapeDtypeStruct(s, d) for s,...  12.9 us
    ppermute x1, waiting for transfers between devices, fast_body(): across_got = lax.ppermute(across, 'lon', swap('lon', 2))  5.64 us
    ppermute x3, starting transfers between devices, fast_body(): lax.ppermute(reduced, 'lon', swap('lon', step))  4.45 us
    ppermute x3, waiting for transfers between devices, fast_body(): lax.ppermute(reduced, 'lon', swap('lon', step))  3.08 us
    ppermute x1, starting transfers between devices, fast_body(): lat_in = lax.ppermute(edge, 'lat', swap('lat', 1))  3.03 us
    ppermute x1, starting transfers between devices, fast_body(): far_got = lax.ppermute(far, 'lon', swap('lon', 3))  2.54 us
    ppermute x1, starting transfers between devices, fast_body(): far_in = lax.ppermute(far, 'lon', swap('lon', 3))  2.47 us
    ppermute x1, starting transfers between devices, fast_body(): near_in = lax.ppermute(near, 'lon', swap('lon', 1))  2.17 us
  transfers between devices with their start and end apart: 15, of which 10 were waited for; matrix products, arithmetic and copies ran while one was open for 0% of the time, Pallas kernels for 18%

profile of v3, /device:TPU:0, one launch (start us, length us, event | category | flops | bytes accessed | tf_op | source)
XLA Modules:
  0.0 49.8 jit_solution(1995531877782092806)
XLA Ops:
  0.6 1.1 %shard_map.203 = (bf16[256,192]{1,0:T(8,128)(2,1)S(1)}, bf16[48,192]{1,0:T(8,128)(2,1)S(1)}, f32[256,192]{1,0:T(8,128)S(1)}) custom-call(bf16[256,192]{1,0:T(8,128)(2,1)} %bitcast.19, s32[16,16]{1,0:T(8,128)} %mask_hbm.1), custom_call_target="tpu_custom_call" | custom-call | bytes 412672 | tf_op jit(solution)/shard_map/pallas_call | solution.py:311
  1.7 3.0 %collective-permute-start = (bf16[48,192]{1,0:T(8,128)(2,1)S(1)}, bf16[48,192]{1,0:T(8,128)(2,1)S(1)}, u32[]{:S(2)}, u32[]{:S(2)}) collective-permute-start(bf16[48,192]{1,0:T(8,128)(2,1)S(1)} %get-tuple-element.59), channel_id=1, source_target_pairs={{0,2},{2,0},{1,3},{3,1},{4,6},{6,4},{5,7},{7,5},{8,10},{10,8},{9,1... | collective-permute-start | bytes 55304 | tf_op jit(solution)/shard_map/ppermute | solution.py:769
  4.7 1.4 %shard_map.204 = (bf16[256,192]{1,0:T(8,128)(2,1)S(1)}, f32[1,192]{1,0:T(1,128)S(1)}, bf16[192,768]{1,0:T(8,128)(2,1)S(1)}, f32[7,7,192]{2,1,0:T(8,128)S(1)}, f3...) custom-call(f32[256,192]{1,0:T(8,128)S(1)} %get-tuple-element.60.ful, ...), custom_call_target="tpu_custom_call" | custom-call | flops 75497472 | bytes 2546688 | tf_op jit(solution)/shard_map/pallas_call | solution.py:311
  6.2 0.4 collective-permute-done.lat_ref
  6.6 0.1 shard_map.205
  6.7 2.2 %collective-permute-start.1 = (bf16[24,768]{1,0:T(8,128)(2,1)S(1)}, bf16[24,768]{1,0:T(8,128)(2,1)S(1)}, u32[]{:S(2)}, u32[]{:S(2)}) collective-permute-start(bf16[24,768]{1,0:T(8,128)(2,1)S(1)} %get-tuple-element.62), channel_id=1, source_target_pairs={{0,4},{4,0},{8,12},{12,8},{1,5},{5,1},{9,13},{13,9},{2,6},{6,2},{1... | collective-permute-start | bytes 110600 | tf_op jit(solution)/shard_map/ppermute | solution.py:790
  8.8 2.5 %collective-permute-start.2 = (bf16[24,768]{1,0:T(8,128)(2,1)S(1)}, bf16[24,768]{1,0:T(8,128)(2,1)S(1)}, u32[]{:S(2)}, u32[]{:S(2)}) collective-permute-start(bf16[24,768]{1,0:T(8,128)(2,1)S(1)} %get-tuple-element.63), channel_id=1, source_target_pairs={{0,12},{4,8},{8,4},{12,0},{1,13},{5,9},{9,5},{13,1},{2,14},{6,10},... | collective-permute-start | bytes 110600 | tf_op jit(solution)/shard_map/ppermute | solution.py:791
  11.3 1.9 %shard_map.206.inner_ref = f32[2,256,128]{2,1,0:T(8,128)S(1)} custom-call(bf16[256,192]{1,0:T(8,128)(2,1)S(1)} %get-tuple-element.58.start_ref, bf16[48,192]{1,0:T(8,128)(2,1)S(1)} %collective-permute-done.lat_ref, f32[7,7,192]{2,1,0:T(8,128)S(1)} %get-tuple-element.64.kernel_ref, f32[1,192]{1,0:T(1,128)S(1)} %get-tuple-element.61.loaded_ref.bias_ref), custom_call_target="tpu_custom_call" | custom-call | flops 4915200 | bytes 417280 | tf_op jit(solution)/shard_map/pallas_call | solution.py:311
  13.2 0.0 collective-permute-done.1.near_ref
  13.2 1.4 %collective-permute-done.2.far_ref = bf16[24,768]{1,0:T(8,128)(2,1)S(1)} collective-permute-done((bf16[24,768]{1,0:T(8,128)(2,1)S(1)}, bf16[24,768]{1,0:T(8,128)(2,1)S(1)}, u32[]{:S(2)}, u32[]{:S(2)}) %collective-permute-start.2) | collective-permute-done | bytes 36896 | tf_op jit(solution)/shard_map/ppermute | solution.py:791
  14.6 1.5 %shard_map.207 = (bf16[192,768]{1,0:T(8,128)(2,1)S(1)}, f32[192,768]{1,0:T(8,128)S(1)}, f32[256,192]{1,0:T(8,128)S(1)}, f32[256,128]{1,0:T(8,128)S(1)}, bf16[256...) custom-call(f32[2,256,128]{2,1,0:T(8,128)S(1)} %shard_map.206.inner_ref, ...), custom_call_target="tpu_custom_call" | custom-call | flops 226492416 | bytes 3559680 | tf_op jit(solution)/shard_map/pallas_call | solution.py:311
  16.1 0.1 collective-permute-start.3
  16.2 0.5 shard_map.208
  16.7 1.1 %collective-permute-done.3.other_ref = bf16[192,768]{1,0:T(8,128)(2,1)S(1)} collective-permute-done((bf16[192,768]{1,0:T(8,128)(2,1)S(1)}, bf16[192,768]{1,0:T(8,128)(2,1)S(1)}, u32[]{:S(2)}, u32[]{:S(2)}) %collective-permute-start.3) | collective-permute-done | bytes 294944 | tf_op jit(solution)/shard_map/ppermute | solution.py:819
  17.8 0.1 shard_map.210
  17.8 1.6 %collective-permute-start.4 = (bf16[112,768]{1,0:T(8,128)(2,1)S(1)}, bf16[112,768]{1,0:T(8,128)(2,1)S(1)}, u32[]{:S(2)}, u32[]{:S(2)}) collective-permute-start(bf16[112,768]{1,0:T(8,128)(2,1)S(1)} %get-tuple-element.86), channel_id=1, source_target_pairs={{0,2},{2,0},{1,3},{3,1},{4,6},{6,4},{5,7},{7,5},{8,10},{10,8},{9,1... | collective-permute-start | bytes 516104 | tf_op jit(solution)/shard_map/ppermute | solution.py:832
  19.4 2.5 %shard_map.209 = (bf16[32,768]{1,0:T(8,128)(2,1)S(1)}, bf16[256,192]{1,0:T(8,128)(2,1)}) custom-call(bf16[256,192]{1,0:T(8,128)(2,1)S(1)} %get-tuple-element.58.start_ref, bf16[48,192]{1,0:T(8,128)(2,1)S(1)} %collective-permute-done.lat_ref, bf16[24,768]{1,0:T(8,128)(2,1)S(1)} %collective-permute-done.1.near_ref, ...), custom_call_target="tpu_custom_call" | custom-call | flops 80412672 | bytes 1524480 | tf_op jit(solution)/shard_map/pallas_call | solution.py:311
  21.9 0.1 collective-permute-start.5
  22.0 1.2 %collective-permute-done.5.small_other_ref = bf16[32,768]{1,0:T(8,128)(2,1)S(1)} collective-permute-done((bf16[32,768]{1,0:T(8,128)(2,1)S(1)}, bf16[32,768]{1,0:T(8,128)(2,1)S(1)}, u32[]{:S(2)}, u32[]{:S(2)}) %collective-permute-start.5) | collective-permute-done | bytes 49184 | tf_op jit(solution)/shard_map/ppermute | solution.py:851
  23.2 1.1 %collective-permute-done.4.lat_ref = bf16[112,768]{1,0:T(8,128)(2,1)S(1)} collective-permute-done((bf16[112,768]{1,0:T(8,128)(2,1)S(1)}, bf16[112,768]{1,0:T(8,128)(2,1)S(1)}, u32[]{:S(2)}, u32[]{:S(2)}) %collective-permute-start.4) | collective-permute-done | bytes 172064 | tf_op jit(solution)/shard_map/ppermute | solution.py:832
  24.3 0.2 shard_map.211
  24.5 0.1 collective-permute-start.6
  24.6 2.5 %collective-permute-start.8 = (bf16[56,768]{1,0:T(8,128)(2,1)S(1)}, bf16[56,768]{1,0:T(8,128)(2,1)S(1)}, u32[]{:S(2)}, u32[]{:S(2)}) collective-permute-start(bf16[56,768]{1,0:T(8,128)(2,1)S(1)} %get-tuple-element.91), channel_id=1, source_target_pairs={{0,12},{4,8},{8,4},{12,0},{1,13},{5,9},{9,5},{13,1},{2,14},{6,10},... | collective-permute-start | bytes 258056 | tf_op jit(solution)/shard_map/ppermute | solution.py:867
  27.1 0.9 %collective-permute-start.7 = (bf16[32,768]{1,0:T(8,128)(2,1)S(1)}, bf16[32,768]{1,0:T(8,128)(2,1)S(1)}, u32[]{:S(2)}, u32[]{:S(2)}) collective-permute-start(bf16[32,768]{1,0:T(8,128)(2,1)S(1)} %get-tuple-element.90), channel_id=1, source_target_pairs={{0,8},{4,12},{8,0},{12,4},{1,9},{5,13},{9,1},{13,5},{2,10},{6,14},... | collective-permute-start | bytes 147464 | tf_op jit(solution)/shard_map/ppermute | solution.py:866
  28.1 5.6 %collective-permute-done.7.across_ref = bf16[32,768]{1,0:T(8,128)(2,1)S(1)} collective-permute-done((bf16[32,768]{1,0:T(8,128)(2,1)S(1)}, bf16[32,768]{1,0:T(8,128)(2,1)S(1)}, u32[]{:S(2)}, u32[]{:S(2)}) %collective-permute-start.7) | collective-permute-done | bytes 49184 | tf_op jit(solution)/shard_map/ppermute | solution.py:866
  33.7 0.0 collective-permute-done.6.near_ref
  33.7 0.0 collective-permute-done.8.far_ref
  33.7 2.3 %collective-permute-start.11 = (bf16[32,768]{1,0:T(8,128)(2,1)S(1)}, bf16[32,768]{1,0:T(8,128)(2,1)S(1)}, u32[]{:S(2)}, u32[]{:S(2)}) collective-permute-start(bf16[32,768]{1,0:T(8,128)(2,1)S(1)} %shard_map.212.own_ref), channel_id=1, source_target_pairs={{0,12},{4,8},{8,4},{12,0},{1,13},{5,9},{9,5},{13,1},{2,14},{6,10},... | collective-permute-start | bytes 147464 | tf_op jit(solution)/shard_map/ppermute | solution.py:875
  36.0 0.0 collective-permute-start.10
  36.0 2.2 %collective-permute-start.9 = (bf16[32,768]{1,0:T(8,128)(2,1)S(1)}, bf16[32,768]{1,0:T(8,128)(2,1)S(1)}, u32[]{:S(2)}, u32[]{:S(2)}) collective-permute-start(bf16[32,768]{1,0:T(8,128)(2,1)S(1)} %shard_map.212.own_ref), channel_id=1, source_target_pairs={{0,4},{4,0},{8,12},{12,8},{1,5},{5,1},{9,13},{13,9},{2,6},{6,2},{1... | collective-permute-start | bytes 147464 | tf_op jit(solution)/shard_map/ppermute | solution.py:875
  38.2 1.8 %collective-permute-done.11.far_ref = bf16[32,768]{1,0:T(8,128)(2,1)S(1)} collective-permute-done((bf16[32,768]{1,0:T(8,128)(2,1)S(1)}, bf16[32,768]{1,0:T(8,128)(2,1)S(1)}, u32[]{:S(2)}, u32[]{:S(2)}) %collective-permute-start.11) | collective-permute-done | bytes 49184 | tf_op jit(solution)/shard_map/ppermute | solution.py:875
  40.0 1.2 %collective-permute-done.10.across_ref = bf16[32,768]{1,0:T(8,128)(2,1)S(1)} collective-permute-done((bf16[32,768]{1,0:T(8,128)(2,1)S(1)}, bf16[32,768]{1,0:T(8,128)(2,1)S(1)}, u32[]{:S(2)}, u32[]{:S(2)}) %collective-permute-start.10) | collective-permute-done | bytes 49184 | tf_op jit(solution)/shard_map/ppermute | solution.py:875
  41.3 0.0 collective-permute-done.9.near_ref
  41.3 1.6 %collective-permute-start.12 = (bf16[128,768]{1,0:T(8,128)(2,1)S(1)}, bf16[128,768]{1,0:T(8,128)(2,1)S(1)}, u32[]{:S(2)}, u32[]{:S(2)}) collective-permute-start(bf16[128,768]{1,0:T(8,128)(2,1)S(1)} %get-tuple-element.92.own_ref), channel_id=1, source_target_pairs={{0,2},{2,0},{1,3},{3,1},{4,6},{6,4},{5,7},{7,5},{8,10},{10,8},{9,1... | collective-permute-start | bytes 589832 | tf_op jit(solution)/shard_map/ppermute | solution.py:891
  42.9 2.6 %shard_map.214 = bf16[256,192]{1,0:T(8,128)(2,1)} custom-call(f32[256,192]{1,0:T(8,128)S(1)} %get-tuple-element.74.conv_grad_ref, bf16[112,768]{1,0:T(8,128)(2,1)S(1)} %collective-permute-done.4.lat_ref, bf16[56,768]{1,0:T(8,128)(2,1)S(1)} %collective-permute-done.6.near_ref, bf16[56,768]{1,0:T(8,128)(2,1)S(1)} %collective-permute-done.8.far_ref, ...), custom_call_target="tpu_custom_call" | custom-call | flops 4915200 | bytes 971520 | tf_op jit(solution)/shard_map/pallas_call | solution.py:311
  45.4 1.6 %collective-permute-done.12.lat_ref = bf16[128,768]{1,0:T(8,128)(2,1)S(1)} collective-permute-done((bf16[128,768]{1,0:T(8,128)(2,1)S(1)}, bf16[128,768]{1,0:T(8,128)(2,1)S(1)}, u32[]{:S(2)}, u32[]{:S(2)}) %collective-permute-start.12) | collective-permute-done | bytes 196640 | tf_op jit(solution)/shard_map/ppermute | solution.py:891
  47.1 0.0 collective-permute-start.14
  47.1 0.5 %collective-permute-start.13 = (bf16[96,768]{1,0:T(8,128)(2,1)S(1)}, bf16[96,768]{1,0:T(8,128)(2,1)S(1)}, u32[]{:S(2)}, u32[]{:S(2)}) collective-permute-start(bf16[96,768]{1,0:T(8,128)(2,1)S(1)} %get-tuple-element.95), channel_id=1, source_target_pairs={{0,1},{1,0},{2,3},{3,2},{4,5},{5,4},{6,7},{7,6},{8,9},{9,8},{10,11... | collective-permute-start | bytes 442376 | tf_op jit(solution)/shard_map/ppermute | solution.py:892
  47.6 1.1 %collective-permute-done.13.dp_own_ref = bf16[96,768]{1,0:T(8,128)(2,1)S(1)} collective-permute-done((bf16[96,768]{1,0:T(8,128)(2,1)S(1)}, bf16[96,768]{1,0:T(8,128)(2,1)S(1)}, u32[]{:S(2)}, u32[]{:S(2)}) %collective-permute-start.13) | collective-permute-done | bytes 147488 | tf_op jit(solution)/shard_map/ppermute | solution.py:892
  48.7 0.0 collective-permute-done.14.dp_lat_ref
  48.7 1.1 %shard_map.215 = (f32[192,768]{1,0:T(8,128)}, f32[192,768]{1,0:T(8,128)}, f32[7,7,192]{2,1,0:T(8,128)}, f32[1,192]{1,0:T(1,128)}, f32[1,192]{1,0:T(1,128)}, /*in...) custom-call(bf16[128,768]{1,0:T(8,128)(2,1)S(1)} %get-tuple-element.92.own_ref, ...), custom_call_target="tpu_custom_call" | custom-call | bytes 1961472 | tf_op jit(solution)/shard_map/pallas_call | solution.py:311
  (2 shorter events, 0.1 us)
Async XLA Ops:
  1.7 4.8 %collective-permute-start = (bf16[48,192]{1,0:T(8,128)(2,1)S(1)}, bf16[48,192]{1,0:T(8,128)(2,1)S(1)}, u32[]{:S(2)}, u32[]{:S(2)}) collective-permute-start(bf16[48,192]{1,0:T(8,128)(2,1)S(1)} %get-tuple-element.59), channel_id=1, source_target_pairs={{0,2},{2,0},{1,3},{3,1},{4,6},{6,4},{5,7},{7,5},{8,10},{10,8},{9,1... | collective-permute-start | bytes 55304 | tf_op jit(solution)/shard_map/ppermute | solution.py:769
  6.7 6.5 %collective-permute-start.1 = (bf16[24,768]{1,0:T(8,128)(2,1)S(1)}, bf16[24,768]{1,0:T(8,128)(2,1)S(1)}, u32[]{:S(2)}, u32[]{:S(2)}) collective-permute-start(bf16[24,768]{1,0:T(8,128)(2,1)S(1)} %get-tuple-element.62), channel_id=1, source_target_pairs={{0,4},{4,0},{8,12},{12,8},{1,5},{5,1},{9,13},{13,9},{2,6},{6,2},{1... | collective-permute-start | bytes 110600 | tf_op jit(solution)/shard_map/ppermute | solution.py:790
  8.8 5.8 %collective-permute-start.2 = (bf16[24,768]{1,0:T(8,128)(2,1)S(1)}, bf16[24,768]{1,0:T(8,128)(2,1)S(1)}, u32[]{:S(2)}, u32[]{:S(2)}) collective-permute-start(bf16[24,768]{1,0:T(8,128)(2,1)S(1)} %get-tuple-element.63), channel_id=1, source_target_pairs={{0,12},{4,8},{8,4},{12,0},{1,13},{5,9},{9,5},{13,1},{2,14},{6,10},... | collective-permute-start | bytes 110600 | tf_op jit(solution)/shard_map/ppermute | solution.py:791
  16.1 1.6 %collective-permute-start.3 = (bf16[192,768]{1,0:T(8,128)(2,1)S(1)}, bf16[192,768]{1,0:T(8,128)(2,1)S(1)}, u32[]{:S(2)}, u32[]{:S(2)}) collective-permute-start(bf16[192,768]{1,0:T(8,128)(2,1)S(1)} %get-tuple-element.84), channel_id=1, source_target_pairs={{0,1},{1,0},{2,3},{3,2},{4,5},{5,4},{6,7},{7,6},{8,9},{9,8},{10,11... | collective-permute-start | bytes 884744 | tf_op jit(solution)/shard_map/ppermute | solution.py:819
  17.8 6.5 %collective-permute-start.4 = (bf16[112,768]{1,0:T(8,128)(2,1)S(1)}, bf16[112,768]{1,0:T(8,128)(2,1)S(1)}, u32[]{:S(2)}, u32[]{:S(2)}) collective-permute-start(bf16[112,768]{1,0:T(8,128)(2,1)S(1)} %get-tuple-element.86), channel_id=1, source_target_pairs={{0,2},{2,0},{1,3},{3,1},{4,6},{6,4},{5,7},{7,5},{8,10},{10,8},{9,1... | collective-permute-start | bytes 516104 | tf_op jit(solution)/shard_map/ppermute | solution.py:832
  21.9 1.3 %collective-permute-start.5 = (bf16[32,768]{1,0:T(8,128)(2,1)S(1)}, bf16[32,768]{1,0:T(8,128)(2,1)S(1)}, u32[]{:S(2)}, u32[]{:S(2)}) collective-permute-start(bf16[32,768]{1,0:T(8,128)(2,1)S(1)} %get-tuple-element.87.small_ref), channel_id=1, source_target_pairs={{0,1},{1,0},{2,3},{3,2},{4,5},{5,4},{6,7},{7,6},{8,9},{9,8},{10,11... | collective-permute-start | bytes 147464 | tf_op jit(solution)/shard_map/ppermute | solution.py:851
  24.5 9.2 %collective-permute-start.6 = (bf16[56,768]{1,0:T(8,128)(2,1)S(1)}, bf16[56,768]{1,0:T(8,128)(2,1)S(1)}, u32[]{:S(2)}, u32[]{:S(2)}) collective-permute-start(bf16[56,768]{1,0:T(8,128)(2,1)S(1)} %get-tuple-element.89), channel_id=1, source_target_pairs={{0,4},{4,0},{8,12},{12,8},{1,5},{5,1},{9,13},{13,9},{2,6},{6,2},{1... | collective-permute-start | bytes 258056 | tf_op jit(solution)/shard_map/ppermute | solution.py:865
  24.6 9.1 %collective-permute-start.8 = (bf16[56,768]{1,0:T(8,128)(2,1)S(1)}, bf16[56,768]{1,0:T(8,128)(2,1)S(1)}, u32[]{:S(2)}, u32[]{:S(2)}) collective-permute-start(bf16[56,768]{1,0:T(8,128)(2,1)S(1)} %get-tuple-element.91), channel_id=1, source_target_pairs={{0,12},{4,8},{8,4},{12,0},{1,13},{5,9},{9,5},{13,1},{2,14},{6,10},... | collective-permute-start | bytes 258056 | tf_op jit(solution)/shard_map/ppermute | solution.py:867
  27.1 6.6 %collective-permute-start.7 = (bf16[32,768]{1,0:T(8,128)(2,1)S(1)}, bf16[32,768]{1,0:T(8,128)(2,1)S(1)}, u32[]{:S(2)}, u32[]{:S(2)}) collective-permute-start(bf16[32,768]{1,0:T(8,128)(2,1)S(1)} %get-tuple-element.90), channel_id=1, source_target_pairs={{0,8},{4,12},{8,0},{12,4},{1,9},{5,13},{9,1},{13,5},{2,10},{6,14},... | collective-permute-start | bytes 147464 | tf_op jit(solution)/shard_map/ppermute | solution.py:866
  33.7 6.3 %collective-permute-start.11 = (bf16[32,768]{1,0:T(8,128)(2,1)S(1)}, bf16[32,768]{1,0:T(8,128)(2,1)S(1)}, u32[]{:S(2)}, u32[]{:S(2)}) collective-permute-start(bf16[32,768]{1,0:T(8,128)(2,1)S(1)} %shard_map.212.own_ref), channel_id=1, source_target_pairs={{0,12},{4,8},{8,4},{12,0},{1,13},{5,9},{9,5},{13,1},{2,14},{6,10},... | collective-permute-start | bytes 147464 | tf_op jit(solution)/shard_map/ppermute | solution.py:875
  36.0 5.3 %collective-permute-start.10 = (bf16[32,768]{1,0:T(8,128)(2,1)S(1)}, bf16[32,768]{1,0:T(8,128)(2,1)S(1)}, u32[]{:S(2)}, u32[]{:S(2)}) collective-permute-start(bf16[32,768]{1,0:T(8,128)(2,1)S(1)} %shard_map.212.own_ref), channel_id=1, source_target_pairs={{0,8},{4,12},{8,0},{12,4},{1,9},{5,13},{9,1},{13,5},{2,10},{6,14},... | collective-permute-start | bytes 147464 | tf_op jit(solution)/shard_map/ppermute | solution.py:875
  36.0 5.3 %collective-permute-start.9 = (bf16[32,768]{1,0:T(8,128)(2,1)S(1)}, bf16[32,768]{1,0:T(8,128)(2,1)S(1)}, u32[]{:S(2)}, u32[]{:S(2)}) collective-permute-start(bf16[32,768]{1,0:T(8,128)(2,1)S(1)} %shard_map.212.own_ref), channel_id=1, source_target_pairs={{0,4},{4,0},{8,12},{12,8},{1,5},{5,1},{9,13},{13,9},{2,6},{6,2},{1... | collective-permute-start | bytes 147464 | tf_op jit(solution)/shard_map/ppermute | solution.py:875
  41.3 5.7 %collective-permute-start.12 = (bf16[128,768]{1,0:T(8,128)(2,1)S(1)}, bf16[128,768]{1,0:T(8,128)(2,1)S(1)}, u32[]{:S(2)}, u32[]{:S(2)}) collective-permute-start(bf16[128,768]{1,0:T(8,128)(2,1)S(1)} %get-tuple-element.92.own_ref), channel_id=1, source_target_pairs={{0,2},{2,0},{1,3},{3,1},{4,6},{6,4},{5,7},{7,5},{8,10},{10,8},{9,1... | collective-permute-start | bytes 589832 | tf_op jit(solution)/shard_map/ppermute | solution.py:891
  47.1 1.7 %collective-permute-start.14 = (bf16[128,768]{1,0:T(8,128)(2,1)S(1)}, bf16[128,768]{1,0:T(8,128)(2,1)S(1)}, u32[]{:S(2)}, u32[]{:S(2)}) collective-permute-start(bf16[128,768]{1,0:T(8,128)(2,1)S(1)} %collective-permute-done.12.lat_ref), channel_id=1, source_target_pairs={{0,1},{1,0},{2,3},{3,2},{4,5},{5,4},{6,7},{7,6},{8,9},{9,8},{10,11... | collective-permute-start | bytes 589832 | tf_op jit(solution)/shard_map/ppermute | solution.py:894
  47.1 1.6 %collective-permute-start.13 = (bf16[96,768]{1,0:T(8,128)(2,1)S(1)}, bf16[96,768]{1,0:T(8,128)(2,1)S(1)}, u32[]{:S(2)}, u32[]{:S(2)}) collective-permute-start(bf16[96,768]{1,0:T(8,128)(2,1)S(1)} %get-tuple-element.95), channel_id=1, source_target_pairs={{0,1},{1,0},{2,3},{3,2},{4,5},{5,4},{6,7},{7,6},{8,9},{9,8},{10,11... | collective-permute-start | bytes 442376 | tf_op jit(solution)/shard_map/ppermute | solution.py:892
